TPU v7x, 32 devices: a whole 2x2x4 slice. The times are simulated.
32 devices in a mesh: dp: 8 (over y, x, core), mp: 4 (over z).
Axes of the slice: x: 2, y: 2, z: 4, core: 2. Of those that a mesh axis runs over, the one named last changes fastest.
Arguments:
- tokens: bfloat16 [20480, 1024], P(('dp', 'mp')), may hold values from -6 to 6
- context: int32 [40], P('dp'), may hold values from 0 to 475, as said below
- timestep: int32 [40], P('dp'), may hold values from 1 to 5000
- time_weight: float32 [1024], replicated, may hold values from -6 to 6
- time_bias: float32 [1024], replicated, may hold values from -3 to 3
- qkv_weight: bfloat16 [3, 1024, 1024], P(None, 'dp', 'mp'), may hold values from -0.1875 to 0.1875
- qv_bias: bfloat16 [16, 128], P('mp', 'dp'), may hold values from -3 to 3
- out_weight: bfloat16 [1024, 1024], P('mp', 'dp'), may hold values from -1 to 1
- out_bias: float32 [1024], replicated, may hold values from -3 to 3
- gain_one: float32 [1024], replicated, may hold values from 0.5 to 1.5
- shift_one: float32 [1024], replicated, may hold values from -3 to 3
- up_weight: bfloat16 [4096, 1024], P('mp', 'dp'), may hold values from -0.1875 to 0.1875
- up_bias: bfloat16 [32, 128], P('mp', 'dp'), may hold values from -3 to 3
- down_weight: bfloat16 [4096, 1024], P('mp', 'dp'), may hold values from -0.09375 to 0.09375
- down_bias: float32 [1024], replicated, may hold values from -3 to 3
- gain_two: float32 [1024], replicated, may hold values from 0.5 to 1.5
- shift_two: float32 [1024], replicated, may hold values from -3 to 3
- cotangent: bfloat16 [20480, 1024], P(('dp', 'mp')), may hold values from -6 to 6
Outputs:
- layer_out: bfloat16 [20480, 1024], P(('dp', 'mp'))
- grad_tokens: float32 [20480, 1024], P(('dp', 'mp'))
- grad_time_weight: float32 [1024], P(('dp', 'mp'))
- grad_time_bias: float32 [1024], P(('dp', 'mp'))
- grad_qkv_weight: float32 [3, 1024, 1024], P(None, 'dp', 'mp')
- grad_qv_bias: float32 [16, 128], P('mp', 'dp')
- grad_out_weight: float32 [1024, 1024], P('mp', 'dp')
- grad_out_bias: float32 [1024], P(('dp', 'mp'))
- grad_gain_one: float32 [1024], P(('dp', 'mp'))
- grad_shift_one: float32 [1024], P(('dp', 'mp'))
- grad_up_weight: float32 [4096, 1024], P('mp', 'dp')
- grad_up_bias: float32 [32, 128], P('mp', 'dp')
- grad_down_weight: float32 [4096, 1024], P('mp', 'dp')
- grad_down_bias: float32 [1024], P(('dp', 'mp'))
- grad_gain_two: float32 [1024], P(('dp', 'mp'))
- grad_shift_two: float32 [1024], P(('dp', 'mp'))
Inputs may be any that keep to these rules, and one draw needn't show every extreme that they name: Sequence b holds context[b] context tokens followed by 25 block tokens; its remaining positions are padding and are never attended to.
All inputs are finite; a program needn't handle non-finite values.
Results may differ from a plain program's by a relative error of at most 0.019.
Values may be sent and summed in bfloat16 or wider, within the bound.
A program may use at most 128 MiB of HBM per device.

v0:
```python
import functools
import math

import jax
import jax.numpy as jnp
from jax import lax
from jax.experimental import pallas as pl
from jax.experimental.pallas import tpu as pltpu
from jax.sharding import PartitionSpec as P

BLOCK = 25
TSTEPS = 5000
LN_EPS = 1e-05
MASKED = -1e30
MESH = pl.DeviceIdType.MESH
BF = jnp.bfloat16
F32 = jnp.float32
PIECES = 12
LANES = 4
ROWS = 256
COLS = 128
VMEM_LIMIT = 62 * 2**20


def dot_nn(left, right):
    return lax.dot_general(left, right, (((1,), (0,)), ((), ())), preferred_element_type=F32)


def dot_nt(left, right):
    return lax.dot_general(left, right, (((1,), (1,)), ((), ())), preferred_element_type=F32)


def dot_tn(left, right):
    return lax.dot_general(left, right, (((0,), (0,)), ((), ())), preferred_element_type=F32)


class Place:
    def __init__(self, outer):
        dp = lax.axis_index("dp")
        self.z = lax.axis_index("mp")
        self.outer = outer
        self.own = lax.div(dp, outer)
        self.rest = lax.rem(dp, outer)
        self.core = lax.rem(self.own, 2)
        self.chip = lax.div(self.own, 2)
        col, row = lax.rem(self.chip, 2), lax.div(self.chip, 2)
        self.side = row * 2 + (1 - col)
        self.over = (1 - row) * 2 + col
        self.diag = (1 - row) * 2 + (1 - col)

    def dev(self, chip, core, z):
        return ((chip * 2 + core) * self.outer + self.rest, z)

    def partner(self):
        return self.dev(self.chip, 1 - self.core, self.z)

    def beside(self):
        return self.dev(self.side, self.core, self.z)

    def across(self):
        return self.dev(self.over, self.core, self.z)

    def along(self, k):
        return self.dev(self.chip, self.core, lax.rem(self.z + k, 4))


def greet(at):
    barrier = pltpu.get_barrier_semaphore()
    peers = [at.partner(), at.beside(), at.across()] + [at.along(k) for k in range(1, 4)]
    for peer in peers:
        pl.semaphore_signal(barrier, inc=1, device_id=peer, device_id_type=MESH)
    pl.semaphore_wait(barrier, len(peers))


def wait_for(ref, sem):
    pltpu.make_async_copy(ref, ref, sem).wait()


def send(src, dst, send_sem, recv_sem, device):
    pltpu.make_async_remote_copy(
        src, dst, send_sem, recv_sem, device_id=device, device_id_type=MESH
    ).start()


def when_in(piece, count, action):
    @pl.when(jnp.logical_and(piece >= 0, piece < count))
    def _():
        action(piece)


def cols_of(lane):
    return pl.ds(pl.multiple_of(lane * COLS, COLS), COLS)


def tile_rows(start, size):
    return pl.ds(pl.multiple_of(start, 128), size)


def norm_rows(values_in):
    average = jnp.mean(values_in, axis=-1, keepdims=True)
    centred = values_in - average
    rstd = lax.rsqrt(jnp.mean(centred * centred, axis=-1, keepdims=True) + LN_EPS)
    return centred * rstd, rstd


def norm_back(grad, xhat, rstd, gain):
    scaled = grad * gain
    first = jnp.mean(scaled, axis=-1, keepdims=True)
    second = jnp.mean(scaled * xhat, axis=-1, keepdims=True)
    return rstd * (scaled - first - xhat * second)


def fold_rows(values_in):
    rows, model = values_in.shape
    return jnp.sum(values_in.reshape(rows // 8, 8, model), axis=0)


def forward_kernel(
    outer, live, shard, small, h, tokens, cotangent, fraction, vecs,
    w_one, w_up, w_down, small_full, h_win_out, q_out, k_out, v_out, attn_out, y_out, hidden_out, slope_out,
    xhat_out, dz_out, grad_f_out, layer_out, lse, rstd_out, sums,
    h_win, q, k, v, attn, y_low, hidden, slope, xhat, acc, pre, grad_f, out_rows, bias_in, bias, wbuf, v_t,
    own_sem, sent, got_z, got_x, got_y, got_xd, got_yd, got_c, halo_sent, halo_got, load_sem, store_sem, slope_sem,
):
    at = Place(outer)
    greet(at)
    z, rows, model = at.z, h.shape[0], h.shape[1]
    step = rows // 5
    groups = (w_one, w_up, w_down)
    x_lane, y_lane, d_lane = at.side * 2 + at.core, at.over * 2 + at.core, at.diag * 2 + at.core

    def source(p):
        return small if p is None else shard.at[pl.ds(p, 1)]

    def block(ref, lane, start, count):
        return ref.at[pl.ds(start, count), :, cols_of(lane)]

    def index(p):
        return PIECES if p is None else p

    def grouped(action):
        def run(p):
            if p is None:
                action(None, small_full)
                return
            if isinstance(p, int):
                action(p, groups[p // 4].at[p % 4])
                return
            for g, ref in enumerate(groups):
                @pl.when(lax.div(p, 4) == g)
                def _():
                    action(p, ref.at[p - 4 * g])

        return run

    def first(p, ref):
        i, src, dst = index(p), source(p), block(ref, at.own, z, 1)
        send(src, dst, sent.at[i], got_x.at[i], at.beside())
        send(src, dst, sent.at[i], got_y.at[i], at.across())
        for step_z in range(1, 4):
            send(src, dst, sent.at[i], got_z.at[i], at.along(step_z))
        send(src, dst, sent.at[i], got_c.at[i], at.partner())

    def second(p, ref):
        i = index(p)
        wait_for(block(ref, at.own, 0, 3), got_z.at[i])
        for step_z in range(1, 4):
            part = block(ref, at.own, lax.rem(z + step_z, 4), 1)
            send(part, part, sent.at[i], got_x.at[i], at.beside())
            send(part, part, sent.at[i], got_y.at[i], at.across())
            send(part, part, sent.at[i], got_c.at[i], at.partner())

    def third(p, ref):
        i = index(p)
        wait_for(block(ref, x_lane, 0, 4), got_x.at[i])
        part = block(ref, x_lane, 0, 2)
        send(part, part, sent.at[i], got_yd.at[i], at.across())
        part = block(ref, x_lane, 0, 4)
        send(part, part, sent.at[i], got_c.at[i], at.partner())
        wait_for(block(ref, y_lane, 0, 4), got_y.at[i])
        part = block(ref, y_lane, 2, 2)
        send(part, part, sent.at[i], got_xd.at[i], at.beside())
        part = block(ref, y_lane, 0, 4)
        send(part, part, sent.at[i], got_c.at[i], at.partner())

    def fourth(p, ref):
        i = index(p)
        wait_for(block(ref, d_lane, 0, 2), got_yd.at[i])
        wait_for(block(ref, d_lane, 2, 2), got_xd.at[i])
        part = block(ref, d_lane, 0, 4)
        send(part, part, sent.at[i], got_c.at[i], at.partner())

    def load(p, ref):
        slot = lax.rem(p, 3)
        return pltpu.make_async_copy(ref, wbuf.at[slot], load_sem.at[slot])

    def fifth(p, ref):
        wait_for(ref.at[:, :, 0 : 4 * COLS], got_c.at[index(p)])
        if p is None:
            pltpu.make_async_copy(small_full, bias_in, own_sem.at[1]).start()
        else:
            load(p, ref).start()

    def drain(p, ref):
        wait_for(ref.at[:, :, 0 : 7 * COLS], sent.at[index(p)])
        wait_for(ref.at[0:3, :, 0:COLS], sent.at[index(p)])

    first, second, third, fourth, fifth, drain = (
        grouped(action) for action in (first, second, third, fourth, fifth, drain)
    )

    def halo():
        for i in range(3):
            @pl.when(jnp.logical_and(z >= 1, z < 4 - i))
            def _():
                dst = h_win.at[tile_rows((4 + z + i) * step, step)]
                send(h.at[tile_rows(i * step, step)], dst, halo_sent, halo_got, at.along(3))

            @pl.when(jnp.logical_and(z <= 2, z >= i))
            def _():
                dst = h_win.at[tile_rows(i * step, step)]
                send(h.at[tile_rows((4 - z + i) * step, step)], dst, halo_sent, halo_got, at.along(1))

    mine = [
        pltpu.make_async_copy(
            shard.at[4 * g : 4 * g + 4], ref.at[:, z, :, cols_of(at.own)], own_sem.at[2 + g]
        )
        for g, ref in enumerate(groups)
    ] + [pltpu.make_async_copy(small, small_full.at[pl.ds(z, 1), :, cols_of(at.own)], own_sem.at[0])]
    stores = []

    def store(src, dst):
        pltpu.make_async_copy(src, dst, store_sem.at[len(stores)]).start()
        stores.append((src, dst))

    n_tiles = model // ROWS

    def tiles(action):
        def run(n, carry):
            action(n, tile_rows(n * ROWS, ROWS))
            return carry

        lax.fori_loop(0, n_tiles, run, 0)

    def weight(p):
        slot = lax.rem(p, 3)
        pltpu.make_async_copy(w_one.at[0], wbuf.at[slot], load_sem.at[slot]).wait()
        return slot

    def make_bias():
        pltpu.make_async_copy(small_full, bias_in, own_sem.at[1]).wait()
        total = bias_in[:, :, 0:COLS].astype(F32)
        for lane in range(1, 8):
            total = total + bias_in[:, :, lane * COLS : (lane + 1) * COLS].astype(F32)
        bias[...] = total

    def project(p, rows_in, target, bias_row):
        slot = weight(p)

        def one(n, span):
            result = dot_nt(rows_in[...], wbuf[slot, n])
            if bias_row is not None:
                result = result + jnp.concatenate(
                    [bias[n, bias_row : bias_row + 1], bias[n, bias_row + 1 : bias_row + 2]], axis=1
                )
            target[:, span] = result.astype(BF)

        tiles(one)

    def queries():
        make_bias()
        project(0, h, q, 8)
        store(q, q_out)

    def keys():
        wait_for(h_win.at[0 : 3 * step], halo_got)
        h_win[tile_rows(z * step, rows), :] = h[...]
        project(1, h_win, k, None)
        store(k, k_out)
        store(h_win, h_win_out)

    def values():
        project(2, h_win, v, 10)
        store(v, v_out)

    def attend_pairs(start, count):
        def pair(i, carry):
            lanes = cols_of(i)
            v_t[...] = v[:, lanes].T
            for j in range(5):
                slot = lax.div(z + j, 4)
                span = tile_rows(slot * 4 * step, 4 * step)
                here = slice(j * step, (j + 1) * step)
                q_two = split_heads(q[here, lanes] * jnp.asarray(0.125, BF))
                scores = masked_scores(k[span, lanes], q_two, jnp.where(slot == 0, live[0], live[1]))
                row_max = jnp.max(scores, axis=0, keepdims=True)
                expo = jnp.exp(scores - row_max)
                total = jnp.sum(expo, axis=0, keepdims=True)
                mixed = dot_nn(v_t[:, span], expo.astype(BF)) / total
                attn[here, lanes] = join_heads(mixed).astype(BF)
                lse[i, j : j + 1, :] = row_max + jnp.log(total)
            return carry

        lax.fori_loop(start, start + count, pair, 0)

    def row_loop(count, action):
        def run(i, carry):
            action(pl.ds(pl.multiple_of(i * count, count), count))
            return carry

        lax.fori_loop(0, rows // count, run, 0)

    def out_project():
        slot = weight(3)

        def one(n, span):
            wide = wbuf[slot, :, :, span].reshape(model, ROWS)
            acc[:, span] = dot_nn(attn[...], wide)

        tiles(one)
        store(attn, attn_out)

        def norm(here):
            h_zero = tokens[here, :].astype(F32) + fraction[here, 0:1] * vecs[0:1, :] + vecs[1:2, :]
            normal, rstd = norm_rows(h_zero + acc[here, :] + vecs[2:3, :])
            xhat[here, :] = normal
            y_low[here, :] = (normal * vecs[3:4, :] + vecs[4:5, :]).astype(BF)
            rstd_out[here, :] = jnp.broadcast_to(rstd, (rstd.shape[0], COLS))

        row_loop(32, norm)
        acc[...] = jnp.zeros_like(acc)
        store(y_low, y_out)
        store(xhat, xhat_out)

    def slope_store(i):
        slot = lax.rem(i, 2)
        return pltpu.make_async_copy(slope.at[slot], slope_out.at[i], slope_sem.at[slot])

    def hidden_store(i):
        return pltpu.make_async_copy(hidden.at[i], hidden_out.at[i], slope_sem.at[2 + i])

    def up_piece(p):
        i, slot = p - 4, weight(p)
        side = lax.rem(i, 2)

        @pl.when(i >= 2)
        def _():
            slope_store(i - 2).wait()

        def one(n, span):
            offset = jnp.concatenate([bias[n, pl.ds(2 * i, 1)], bias[n, pl.ds(2 * i + 1, 1)]], axis=1)
            pre[...] = dot_nt(y_low[...], wbuf[slot, n]) + offset

            def gelu(here):
                x = pre[here, :]
                cdf = 0.5 + 0.5 * lax.erf(x * math.sqrt(0.5))
                pdf = jnp.exp(x * x * -0.5) * (1.0 / math.sqrt(2.0 * math.pi))
                hidden[i, here, span] = (x * cdf).astype(BF)
                slope[side, here, span] = (cdf + x * pdf).astype(BF)

            row_loop(32, gelu)

        tiles(one)
        slope_store(i).start()
        hidden_store(i).start()

    def down_piece(p):
        i, slot = p - 8, weight(p)

        def one(n, span):
            wide = wbuf[slot, :, :, span].reshape(model, ROWS)
            acc[:, span] += dot_nn(hidden[i], wide)

        tiles(one)

    def finish():
        sums[...] = jnp.zeros_like(sums)

        def norm(here):
            y_one = xhat[here, :] * vecs[3:4, :] + vecs[4:5, :]
            normal, rstd = norm_rows(y_one + acc[here, :] + vecs[5:6, :])
            out_rows[here, :] = (normal * vecs[6:7, :] + vecs[7:8, :]).astype(BF)
            cot = cotangent[here, :].astype(F32)
            grad = norm_back(cot, normal, rstd, vecs[6:7, :])
            acc[here, :] = grad
            low = grad.astype(BF)
            grad_f[here, :] = low
            sums[0] += fold_rows(cot * normal)
            sums[1] += fold_rows(cot)
            sums[2] += fold_rows(low.astype(F32))

        row_loop(32, norm)
        store(acc, dz_out)
        store(grad_f, grad_f_out)
        store(out_rows, layer_out)

    first(None)
    first(0)
    first(1)
    halo()
    for copy in mine:
        copy.start()
    stages = ((second, 0), (third, -1), (fourth, -2), (fifth, -3))
    work = {
        4: (queries,),
        5: (keys,),
        6: (values, lambda: attend_pairs(0, 2)),
        7: (lambda: attend_pairs(2, 4),),
        8: (lambda: attend_pairs(6, 2), out_project),
    }

    def tick(t, carry):
        @pl.when(t == 3)
        def _():
            for copy in mine:
                copy.wait()

        for action, shift in ((first, 2),) + stages:
            when_in(t + shift, PIECES, action)
        for action, shift in stages:
            @pl.when(t == -shift)
            def _():
                action(None)
        for when, actions in work.items():
            @pl.when(t == when)
            def _():
                for action in actions:
                    action()

        @pl.when(jnp.logical_and(t >= 9, t < 13))
        def _():
            up_piece(t - 5)

        @pl.when(t >= 13)
        def _():
            down_piece(t - 5)

        return carry

    lax.fori_loop(0, PIECES + 5, tick, 0)
    finish()
    middle = jnp.logical_and(z >= 1, z <= 2)

    @pl.when(middle)
    def _():
        wait_for(h.at[0 : 5 * step], halo_sent)

    @pl.when(jnp.logical_not(middle))
    def _():
        wait_for(h.at[0:step], halo_sent)

    def drain_one(p, carry):
        drain(p)
        return carry

    lax.fori_loop(0, PIECES, drain_one, 0)
    drain(None)
    slope_store(2).wait()
    slope_store(3).wait()
    for i in range(4):
        hidden_store(i).wait()
    for i, (src, dst) in enumerate(stores):
        pltpu.make_async_copy(src, dst, store_sem.at[i]).wait()


def forward_pass(outer, live, shard, small, h, tokens, cotangent, fraction, vecs):
    sem = pltpu.SemaphoreType.DMA
    rows, model = h.shape
    win = rows // 5 * 8
    weights = jax.ShapeDtypeStruct((4, 4, ROWS, model), BF)
    own = jax.ShapeDtypeStruct((rows, model), BF)
    own_wide = jax.ShapeDtypeStruct((rows, model), F32)
    window = jax.ShapeDtypeStruct((win, model), BF)
    tall = jax.ShapeDtypeStruct((4, rows, model), BF)
    anywhere, vmem = pl.BlockSpec(memory_space=pl.ANY), pl.BlockSpec(memory_space=pltpu.VMEM)
    return pl.pallas_call(
        functools.partial(forward_kernel, outer),
        out_shape=(
            weights, weights, weights, jax.ShapeDtypeStruct((4, 16, model), BF),
            window, own, window, window, own, own, tall, tall, own_wide, own_wide, own, own,
            jax.ShapeDtypeStruct((8, 8, 2 * rows // 5), F32),
            jax.ShapeDtypeStruct((rows, COLS), F32),
            jax.ShapeDtypeStruct((3, 8, model), F32),
        ),
        in_specs=[pl.BlockSpec(memory_space=pltpu.SMEM)] + [vmem] * 7,
        out_specs=[anywhere] * 16 + [vmem] * 3,
        scratch_shapes=[
            pltpu.VMEM((win, model), BF),
            pltpu.VMEM((rows, model), BF),
            pltpu.VMEM((win, model), BF),
            pltpu.VMEM((win, model), BF),
            pltpu.VMEM((rows, model), BF),
            pltpu.VMEM((rows, model), BF),
            pltpu.VMEM((4, rows, model), BF),
            pltpu.VMEM((2, rows, model), BF),
            pltpu.VMEM((rows, model), F32),
            pltpu.VMEM((rows, model), F32),
            pltpu.VMEM((rows, ROWS), F32),
            pltpu.VMEM((rows, model), BF),
            pltpu.VMEM((rows, model), BF),
            pltpu.VMEM((4, 16, model), BF),
            pltpu.VMEM((4, 16, COLS), F32),
            pltpu.VMEM((3, 4, ROWS, model), BF),
            pltpu.VMEM((COLS, win), BF),
            sem((5,)),
        ]
        + [sem((PIECES + 1,))] * 7
        + [sem, sem, sem((3,)), sem((10,)), sem((6,))],
        compiler_params=pltpu.CompilerParams(
            collective_id=1, has_side_effects=True, vmem_limit_bytes=VMEM_LIMIT
        ),
        name="forward",
    )(live, shard, small, h, tokens, cotangent, fraction, vecs)


def split_heads(rows):
    low = lax.broadcasted_iota(jnp.int32, rows.shape, 1) < rows.shape[1] // 2
    zero = jnp.zeros_like(rows)
    return jnp.concatenate([jnp.where(low, rows, zero), jnp.where(low, zero, rows)], axis=0)


def join_heads(both):
    half = both.shape[1] // 2
    low = lax.broadcasted_iota(jnp.int32, (both.shape[0], half), 0) < both.shape[0] // 2
    return jnp.where(low, both[:, :half], both[:, half:]).T


def masked_scores(keys, q_two, live):
    scores = dot_nt(keys, q_two)
    return jnp.where(lax.broadcasted_iota(jnp.int32, scores.shape, 0) < live, scores, MASKED)


def backward_kernel(
    outer, live, portion, w_one, w_up, w_down, h_win_in, q_in, k_in, v_in, attn_in, y_in, hidden_in, slope_in,
    xhat_in, dz_in, grad_f_in, lse, rstd, vecs, sums_in,
    out, sums_out, tokens_out, pieces,
    part, lane, got_c, got_dx, got_dy, got_x, got_y, got_z,
    wbuf, hidden, slope, y_low, grad_f, acc, xhat, attn, q, k, v, h_win, dk_acc, dv_acc, k_t, dh_low, halo_in,
    dtile, wide_tile, stage, stats, s_sum, s_got,
    part_sem, sent0, sent1, sent2, sent3, sem_c, sem_dx, sem_dy, sem_x, sem_y, sem_z,
    in_sem, hidden_sem, weight_sem, stage_sem, token_sem, halo_sent, halo_got, small_sent, small_got, credit,
):
    at = Place(outer)
    greet(at)
    z, rows, model = at.z, q.shape[0], q.shape[1]
    step = rows // 5
    n_tiles = model // ROWS

    inputs = [
        (grad_f_in, grad_f), (y_in, y_low), (dz_in, acc), (xhat_in, xhat), (attn_in, attn),
        (q_in, q), (k_in, k), (v_in, v), (h_win_in, h_win),
    ]

    def get(i):
        src, dst = inputs[i]
        return pltpu.make_async_copy(src, dst, in_sem.at[i])

    def get_hidden(i):
        slot = lax.rem(i, 2)
        return (
            pltpu.make_async_copy(hidden_in.at[i], hidden.at[slot], hidden_sem.at[slot]),
            pltpu.make_async_copy(slope_in.at[i], slope.at[slot], hidden_sem.at[2 + slot]),
        )

    def get_weight(ref, slot):
        return pltpu.make_async_copy(ref, wbuf.at[slot], weight_sem.at[slot])

    def put_piece(p):
        return pltpu.make_async_copy(stage, pieces.at[p], stage_sem)

    def get_part(p):
        slot = lax.rem(p, 2)
        return pltpu.make_async_copy(pieces.at[p], part.at[slot], part_sem.at[slot])

    def first(p):
        slot = lax.rem(p, 2)
        get_part(p).wait()

        @pl.when(p >= 2)
        def _():
            pl.semaphore_wait(credit, 1)

        for a in range(4):
            src = part.at[slot, :, :, cols_of(a * 2 + 1 - at.core)]
            send(src, got_c.at[slot, a], sent0.at[p], sem_c.at[p], at.partner())

    def second(p):
        slot, row = lax.rem(p, 2), lax.rem(p, LANES)
        wait_for(got_c.at[slot], sem_c.at[p])

        @pl.when(p >= LANES)
        def _():
            wait_for(lane.at[row, 0], sent1.at[p - LANES])
            wait_for(lane.at[row, 0:2], sent2.at[p - LANES])
            wait_for(lane.at[row, 0, 0:3], sent3.at[p - LANES])

        def add(i, carry):
            a, b = lax.div(i, 4), lax.rem(i, 4)
            lane[row, a, b] = part[slot, b, :, cols_of(a * 2 + at.core)] + got_c[slot, a, b]
            return carry

        lax.fori_loop(0, 16, add, 0)

        @pl.when(p < PIECES - 2)
        def _():
            pl.semaphore_signal(credit, inc=1, device_id=at.partner(), device_id_type=MESH)

        wait_for(got_c.at[slot], sent0.at[p])
        send(lane.at[row, at.diag, 0:2], got_dy.at[p], sent1.at[p], sem_dy.at[p], at.across())
        send(lane.at[row, at.diag, 2:4], got_dx.at[p], sent1.at[p], sem_dx.at[p], at.beside())

    def third(p):
        row = lax.rem(p, LANES)
        wait_for(got_dy.at[p], sem_dy.at[p])

        def add_y(i, carry):
            lane[row, at.side, i] = lane[row, at.side, i] + got_dy[p, i]
            return carry

        lax.fori_loop(0, 2, add_y, 0)
        send(lane.at[row, at.side], got_x.at[p], sent2.at[p], sem_x.at[p], at.beside())
        wait_for(got_dx.at[p], sem_dx.at[p])

        def add_x(i, carry):
            lane[row, at.over, i + 2] = lane[row, at.over, i + 2] + got_dx[p, i]
            return carry

        lax.fori_loop(0, 2, add_x, 0)
        send(lane.at[row, at.over], got_y.at[p], sent2.at[p], sem_y.at[p], at.across())

    def fourth(p):
        row = lax.rem(p, LANES)
        wait_for(got_x.at[p], sem_x.at[p])
        wait_for(got_y.at[p], sem_y.at[p])

        def add(i, carry):
            total = lane[row, at.chip, i].astype(F32) + got_x[p, i].astype(F32)
            lane[row, at.chip, i] = (total + got_y[p, i].astype(F32)).astype(BF)
            return carry

        lax.fori_loop(0, 4, add, 0)
        for far in range(1, 4):
            block = lane.at[row, at.chip, lax.rem(z + far, 4)]
            send(block, got_z.at[p, far - 1], sent3.at[p], sem_z.at[p], at.along(far))

    def fifth(p):
        row = lax.rem(p, LANES)
        wait_for(got_z.at[p], sem_z.at[p])
        total = lane[row, at.chip, z].astype(F32)
        for far in range(3):
            total = total + got_z[p, far].astype(F32)

        @pl.when(p < 8)
        def _():
            out[lax.rem(p, 2) * 4 + lax.div(p, 2)] = total

        @pl.when(p == 8)
        def _():
            out[8] = total

        @pl.when(p > 8)
        def _():
            out[20 - p] = total

    def tiles(action):
        def run(n, carry):
            action(n, tile_rows(n * ROWS, ROWS))
            return carry

        lax.fori_loop(0, n_tiles, run, 0)

    def row_loop(count, action):
        def run(i, carry):
            action(pl.ds(pl.multiple_of(i * count, count), count))
            return carry

        lax.fori_loop(0, rows // count, run, 0)

    def produce(p, left, right):
        def one(n, span):
            stage[n] = dot_tn(left[:, span], right()).astype(BF)

        tiles(one)
        put_piece(p).start()

    def grad_down(i):
        @pl.when(i == 0)
        def _():
            get(0).wait()

        for copy in get_hidden(i):
            copy.wait()

        @pl.when(i > 0)
        def _():
            put_piece(2 * i - 1).wait()

        produce(2 * i, hidden.at[lax.rem(i, 2)], lambda: grad_f[...])

    def grad_pre(i):
        slot = lax.rem(i, 2)
        get_weight(w_down.at[i], 0).wait()

        def one(n, span):
            dtile[...] = dot_nt(grad_f[...], wbuf[0, n])
            stats[8 + i, :, span] = jnp.zeros((8, ROWS), F32)

            def scale(here):
                low = (dtile[here, :] * slope[slot, here, span].astype(F32)).astype(BF)
                slope[slot, here, span] = low
                stats[8 + i, :, span] += fold_rows(low.astype(F32))

            row_loop(64, scale)

        tiles(one)

        @pl.when(i < 3)
        def _():
            get_weight(w_down.at[lax.rem(i + 1, 4)], 0).start()

        @pl.when(i == 3)
        def _():
            get_weight(w_one.at[3], 0).start()

    def grad_up(i):
        @pl.when(i == 0)
        def _():
            get(1).wait()

        put_piece(2 * i).wait()
        produce(2 * i + 1, slope.at[lax.rem(i, 2)], lambda: y_low[...])

    def grad_y(i):
        slot = lax.rem(i, 2)
        get_weight(w_up.at[i], 1).wait()

        @pl.when(i == 0)
        def _():
            get(2).wait()

        def one(n, span):
            wide = wbuf[1, :, :, span].reshape(model, ROWS)
            acc[:, span] += dot_nn(slope[slot], wide)

        tiles(one)

        @pl.when(i < 3)
        def _():
            get_weight(w_up.at[lax.rem(i + 1, 4)], 1).start()

        @pl.when(i == 3)
        def _():
            get_weight(w_one.at[1], 1).start()

        @pl.when(i < 2)
        def _():
            for copy in get_hidden(i + 2):
                copy.start()

    def feed_forward(u):
        i, kind = lax.div(u, 4), lax.rem(u, 4)
        for which, action in enumerate((grad_down, grad_pre, grad_up, grad_y)):
            @pl.when(kind == which)
            def _():
                action(i)

    def norm_one():
        get(3).wait()
        get(4).wait()
        stats[2] = jnp.zeros_like(stats[2])
        stats[3] = jnp.zeros_like(stats[2])
        stats[4] = jnp.zeros_like(stats[2])

        def back(here):
            grad, normal = acc[here, :], xhat[here, :]
            stats[3] += fold_rows(grad * normal)
            stats[4] += fold_rows(grad)
            grad = norm_back(grad, normal, rstd[here, 0:1], vecs[3:4, :])
            acc[here, :] = grad
            low = grad.astype(BF)
            grad_f[here, :] = low
            stats[2] += fold_rows(low.astype(F32))

        row_loop(32, back)
        put_piece(7).wait()
        produce(8, attn, lambda: grad_f[...])
        get_weight(w_one.at[3], 0).wait()

        def one(n, span):
            y_low[:, span] = dot_nt(grad_f[...], wbuf[0, n]).astype(BF)

        tiles(one)
        get_weight(w_one.at[2], 0).start()
        put_piece(8).wait()
        for i in range(5, 9):
            get(i).wait()

    def attend_pairs(start, count):
        def pair(i, carry):
            lanes = cols_of(i)
            k_t[...] = k[:, lanes].T
            dk_acc[...] = jnp.zeros_like(dk_acc)
            dv_acc[...] = jnp.zeros_like(dv_acc)
            total = jnp.zeros((8, COLS), F32)
            for j in range(5):
                slot = lax.div(z + j, 4)
                span = tile_rows(slot * 4 * step, 4 * step)
                here = slice(j * step, (j + 1) * step)
                q_two = split_heads(q[here, lanes] * jnp.asarray(0.125, BF))
                g_two = split_heads(y_low[here, lanes])
                scores = masked_scores(k[span, lanes], q_two, jnp.where(slot == 0, live[0], live[1]))
                probs = jnp.exp(scores - lse[i, j : j + 1, :])
                dv_acc[span, :] += dot_nn(probs.astype(BF), g_two)
                grad_p = dot_nt(v[span, lanes], g_two)
                inner = jnp.sum(probs * grad_p, axis=0, keepdims=True)
                grad_s = (probs * (grad_p - inner)).astype(BF)
                dk_acc[span, :] += dot_nn(grad_s, q_two)
                low = (join_heads(dot_nn(k_t[:, span], grad_s)) * 0.125).astype(BF)
                q[here, lanes] = low
                total = total + fold_rows(low.astype(F32))
            stats[12, :, lanes] = total
            low = dv_acc[...].astype(BF)
            v[:, lanes] = low
            stats[13, :, lanes] = fold_rows(low.astype(F32))
            k[:, lanes] = dk_acc[...].astype(BF)
            return carry

        lax.fori_loop(start, start + count, pair, 0)

    def grad_value():
        produce(9, v, lambda: h_win[...])
        put_piece(9).wait()

    def grad_key_query():
        produce(10, k, lambda: h_win[...])
        put_piece(10).wait()
        produce(11, q, lambda: h_win[tile_rows(z * step, rows), :])

    def share(slot):
        return jnp.where(slot == 0, portion[0], portion[1])

    def input_window():
        get_weight(w_one.at[1], 1).wait()
        get_weight(w_one.at[2], 0).wait()

        def one(n, span):
            wide_k = wbuf[1, :, :, span].reshape(model, ROWS)
            wide_v = wbuf[0, :, :, span].reshape(model, ROWS)
            wide_tile[...] = dot_nn(k[...], wide_k) + dot_nn(v[...], wide_v)
            dh_low[:, span] = wide_tile[...].astype(BF)
            low = fold_rows(wide_tile[0 : 4 * step, :])
            high = fold_rows(wide_tile[4 * step : 8 * step, :])
            stats[0, :, span] = low * portion[0] + high * portion[1]
            stats[1, :, span] = low + high

        tiles(one)
        get_weight(w_one.at[0], 1).start()
        put_piece(11).wait()

        for i in range(3):
            @pl.when(z > i)
            def _():
                src = dh_low.at[tile_rows(i * step, step)]
                dst = halo_in.at[tile_rows((5 - z + i) * step, step)]
                send(src, dst, halo_sent, halo_got, at.along(3))

            @pl.when(z < 3 - i)
            def _():
                src = dh_low.at[tile_rows((5 + z + i) * step, step)]
                dst = halo_in.at[tile_rows(i * step, step)]
                send(src, dst, halo_sent, halo_got, at.along(1))

    def input_own():
        get_weight(w_one.at[0], 1).wait()

        def one(n, span):
            acc[:, span] += dot_nn(q[...], wbuf[1, :, :, span].reshape(model, ROWS))
            for j in range(5):
                total = fold_rows(acc[j * step : (j + 1) * step, span])
                stats[0, :, span] += total * share(lax.div(z + j, 4))
                stats[1, :, span] += total

        tiles(one)
        for i, row in ((5, 2), (6, 0), (7, 1)):
            stats[i] = sums_in[row]
        for i in range(14):
            s_sum[0, i : i + 1, :] = jnp.sum(stats[i], axis=0, keepdims=True)
        s_sum[0, 14:16, :] = jnp.zeros((2, model), F32)

    small_peers = (at.partner, at.beside, at.across)

    def small_send(i):
        send(s_sum.at[i], s_got.at[i], small_sent.at[i], small_got.at[i], small_peers[i]())

    def small_add(i):
        wait_for(s_got.at[i], small_got.at[i])
        s_sum[i + 1] = s_sum[i] + s_got[i]

    def small_spread():
        for far in range(1, 4):
            send(s_sum.at[3], s_got.at[2 + far], small_sent.at[3], small_got.at[3], at.along(far))

    middle = jnp.logical_and(z >= 1, z <= 2)

    def put_tokens(j):
        block = slice(j * step, (j + 1) * step)
        return pltpu.make_async_copy(acc.at[block], tokens_out.at[block], token_sem.at[j])

    def finish_tokens():
        @pl.when(middle)
        def _():
            wait_for(halo_in.at[0 : 5 * step], halo_got)

        @pl.when(jnp.logical_not(middle))
        def _():
            wait_for(halo_in.at[0:step], halo_got)

        for j in range(5):
            block = slice(j * step, (j + 1) * step)
            acc[block, :] += dh_low[tile_rows((z + j) * step, step), :].astype(F32)
            upper = jnp.logical_and(z <= 2, j >= 4 - z)
            lower = jnp.logical_and(z >= 1, j < 4 - z)

            @pl.when(jnp.logical_or(upper, lower))
            def _():
                acc[block, :] += halo_in[block, :].astype(F32)

            put_tokens(j).start()

    get(0).start()
    for i in range(2):
        for copy in get_hidden(i):
            copy.start()
    get_weight(w_down.at[0], 0).start()
    for i in range(1, 3):
        get(i).start()
    get_weight(w_up.at[0], 1).start()
    for i in range(3, 9):
        get(i).start()
    work = {
        5: (norm_one,),
        6: (lambda: attend_pairs(0, 2),),
        7: (lambda: attend_pairs(2, 2),),
        8: (lambda: attend_pairs(4, 2),),
        9: (lambda: attend_pairs(6, 2), grad_value),
        10: (grad_key_query,),
        11: (input_window,),
        12: (input_own, lambda: small_send(0)),
        13: (lambda: small_add(0), lambda: small_send(1)),
        14: (lambda: small_add(1), lambda: small_send(2), finish_tokens),
        15: (lambda: small_add(2), small_spread),
    }

    def slot_run(s, carry):
        c = s - 1
        when_in(c, PIECES, lambda p: get_part(p).start())
        for action, shift in ((second, 1), (third, 2), (fourth, 3), (fifth, 4), (first, 0)):
            when_in(c - shift, PIECES, action)

        @pl.when(s < 6)
        def _():
            def sub_step(u, inner):
                when_in(3 * s + u, 16, feed_forward)
                return inner

            lax.fori_loop(0, 3, sub_step, 0)

        for when, actions in work.items():
            @pl.when(s == when)
            def _():
                for action in actions:
                    action()

        return carry

    lax.fori_loop(0, PIECES + 5, slot_run, 0)
    wait_for(s_got.at[3:6], small_got.at[3])
    sums_out[...] = s_sum[3] + s_got[3] + s_got[4] + s_got[5]
    for p in range(PIECES - LANES, PIECES):
        row = p % LANES
        wait_for(lane.at[row, 0], sent1.at[p])
        wait_for(lane.at[row, 0:2], sent2.at[p])
        wait_for(lane.at[row, 0, 0:3], sent3.at[p])
    for i in range(3):
        wait_for(s_sum.at[i], small_sent.at[i])
    wait_for(s_got.at[0:3], small_sent.at[3])
    wait_for(dh_low.at[0 : 3 * step], halo_sent)
    for j in range(5):
        put_tokens(j).wait()


def backward_pass(outer, live, portion, *arrays):
    sem = pltpu.SemaphoreType.DMA
    model = 8 * COLS
    rows = arrays[4].shape[0]
    win = rows // 5 * 8
    half = (4, 4, ROWS, COLS)
    anywhere, vmem = pl.BlockSpec(memory_space=pl.ANY), pl.BlockSpec(memory_space=pltpu.VMEM)
    return pl.pallas_call(
        functools.partial(backward_kernel, outer),
        out_shape=(
            jax.ShapeDtypeStruct((PIECES, ROWS, COLS), F32),
            jax.ShapeDtypeStruct((16, model), F32),
            jax.ShapeDtypeStruct((rows, model), F32),
            jax.ShapeDtypeStruct((PIECES, 4, ROWS, model), BF),
        ),
        in_specs=[pl.BlockSpec(memory_space=pltpu.SMEM)] * 2 + [anywhere] * 14 + [vmem] * 4,
        out_specs=[vmem, vmem, anywhere, anywhere],
        scratch_shapes=[
            pltpu.VMEM((2, 4, ROWS, model), BF),
            pltpu.VMEM((LANES,) + half, BF),
            pltpu.VMEM((2,) + half, BF),
            pltpu.VMEM((PIECES, 2, ROWS, COLS), BF),
            pltpu.VMEM((PIECES, 2, ROWS, COLS), BF),
            pltpu.VMEM((PIECES, 4, ROWS, COLS), BF),
            pltpu.VMEM((PIECES, 4, ROWS, COLS), BF),
            pltpu.VMEM((PIECES, 3, ROWS, COLS), BF),
            pltpu.VMEM((2, 4, ROWS, model), BF),
            pltpu.VMEM((2, rows, model), BF),
            pltpu.VMEM((2, rows, model), BF),
            pltpu.VMEM((rows, model), BF),
            pltpu.VMEM((rows, model), BF),
            pltpu.VMEM((rows, model), F32),
            pltpu.VMEM((rows, model), F32),
            pltpu.VMEM((rows, model), BF),
            pltpu.VMEM((rows, model), BF),
            pltpu.VMEM((win, model), BF),
            pltpu.VMEM((win, model), BF),
            pltpu.VMEM((win, model), BF),
            pltpu.VMEM((win, COLS), F32),
            pltpu.VMEM((win, COLS), F32),
            pltpu.VMEM((COLS, win), BF),
            pltpu.VMEM((win, model), BF),
            pltpu.VMEM((rows, model), BF),
            pltpu.VMEM((rows, ROWS), F32),
            pltpu.VMEM((win, ROWS), F32),
            pltpu.VMEM((4, ROWS, model), BF),
            pltpu.VMEM((14, 8, model), F32),
            pltpu.VMEM((4, 16, model), F32),
            pltpu.VMEM((6, 16, model), F32),
            sem((2,)),
        ]
        + [sem((PIECES,))] * 10
        + [
            sem((9,)), sem((4,)), sem((2,)), sem, sem((5,)), sem, sem, sem((4,)), sem((4,)),
            pltpu.SemaphoreType.REGULAR,
        ],
        compiler_params=pltpu.CompilerParams(
            collective_id=2, has_side_effects=True, vmem_limit_bytes=VMEM_LIMIT
        ),
        name="backward",
    )(live, portion, *arrays)


def body(
    outer, tokens, context, timestep, time_weight, time_bias, qkv_weight, qv_bias, out_weight, out_bias,
    gain_one, shift_one, up_weight, up_bias, down_weight, down_bias, gain_two, shift_two, cotangent,
):
    z = lax.axis_index("mp")
    rows, model = tokens.shape
    seqs = context.shape[0]
    seq_len = rows * 4 // seqs
    step = rows // 5
    groups = None
    if outer > 1:
        groups = [[i * outer + j for j in range(outer)] for i in range(8)]
        qkv_weight, out_weight, up_weight, down_weight, qv_bias, up_bias = (
            lax.all_gather(w, "dp", axis=1, tiled=True, axis_index_groups=groups)
            for w in (qkv_weight, out_weight, up_weight, down_weight, qv_bias, up_bias)
        )
    shard = jnp.concatenate(
        [
            qkv_weight.transpose(0, 2, 1),
            out_weight.reshape(1, ROWS, COLS),
            up_weight.reshape(4, ROWS, COLS),
            down_weight.reshape(4, ROWS, COLS),
        ]
    )
    own = lax.div(lax.axis_index("dp"), outer)
    n_up, n_qv = up_bias.size, qv_bias.size
    part = jnp.arange(COLS) // up_bias.shape[1]
    up_rows = jnp.where(part == own, jnp.tile(up_bias, (1, 8)), 0)
    qv_rows = jnp.where(part[:64] == own % 4, jnp.tile(qv_bias, (1, 4)), 0).reshape(2, COLS)
    none = jnp.zeros_like(qv_rows)
    q_rows, v_rows = jnp.where(own < 4, qv_rows, none), jnp.where(own < 4, none, qv_rows)
    small = jnp.concatenate([up_rows, q_rows, v_rows, none, none]).reshape(1, 16, COLS)
    row_ids = z * rows + jnp.arange(rows, dtype=jnp.int32)
    owner = (row_ids // seq_len)[:, None] == jnp.arange(seqs, dtype=jnp.int32)[None, :]
    portion = timestep.astype(F32) / TSTEPS
    fraction = jnp.sum(jnp.where(owner, portion[None, :], 0.0), axis=1)
    h_low = (tokens.astype(F32) + fraction[:, None] * time_weight + time_bias).astype(BF)
    live = lax.dynamic_slice((context + BLOCK).astype(jnp.int32), (z,), (2,))
    vecs = jnp.stack(
        [time_weight, time_bias, out_bias, gain_one, shift_one, down_bias, gain_two, shift_two]
    )
    (
        w_one, w_up, w_down, _, h_win, queries, keys, values, attn, y_low, hidden, slope, xhat, grad_z2,
        grad_f, layer_out, lse, rstd, sums,
    ) = forward_pass(
        outer, live, shard, small, h_low, tokens, cotangent,
        jnp.broadcast_to(fraction[:, None], (rows, COLS)), vecs,
    )
    done, totals, grad_tokens, _ = backward_pass(
        outer, live, lax.dynamic_slice(portion, (z,), (2,)), w_one, w_up, w_down, h_win, queries, keys,
        values, attn, y_low, hidden, slope, xhat, grad_z2, grad_f, lse, rstd, vecs, sums,
    )
    weight_grads = [
        done[9:12].transpose(0, 2, 1), done[8], done[4:8].reshape(4 * ROWS, COLS),
        done[0:4].reshape(4 * ROWS, COLS),
    ]
    if outer > 1:
        weight_grads = [
            lax.psum_scatter(g, "dp", scatter_dimension=1, tiled=True, axis_index_groups=groups)
            for g in weight_grads
        ]
        totals = lax.psum(totals, "dp", axis_index_groups=groups)
    grad_qkv, grad_out_w, grad_up, grad_down = weight_grads
    dp = lax.axis_index("dp")
    size = lax.axis_size("dp")
    spread = model // (4 * size)
    vectors = lax.dynamic_slice(totals, (0, (dp * 4 + z) * spread), (8, spread))
    grad_up_bias = lax.dynamic_slice(totals, (8, z * ROWS), (4, ROWS)).reshape(8, COLS)
    grad_up_bias = lax.dynamic_slice(grad_up_bias, (0, dp * (COLS // size)), (8, COLS // size))
    grad_qv_bias = totals[12:14].reshape(2, 16, 64).transpose(1, 0, 2).reshape(16, 2 * 64)
    grad_qv_bias = lax.dynamic_slice(grad_qv_bias, (z * 4, dp * (COLS // size)), (4, COLS // size))
    return (
        layer_out, grad_tokens, vectors[0], vectors[1], grad_qkv, grad_qv_bias,
        grad_out_w, vectors[2], vectors[3], vectors[4], grad_up, grad_up_bias,
        grad_down, vectors[5], vectors[6], vectors[7],
    )


def solution(mesh):
    outer = mesh.shape["dp"] // 8
    placed = (
        P(("dp", "mp"), None), P("dp"), P("dp"), P(), P(), P(None, "dp", "mp"), P("mp", "dp"), P("mp", "dp"),
        P(), P(), P(), P("mp", "dp"), P("mp", "dp"), P("mp", "dp"), P(), P(), P(), P(("dp", "mp"), None),
    )
    spread = P(("dp", "mp"))
    wide = P("mp", "dp")
    return jax.shard_map(
        functools.partial(body, outer),
        mesh=mesh,
        in_specs=placed,
        out_specs=(
            P(("dp", "mp"), None), P(("dp", "mp"), None), spread, spread, P(None, "dp", "mp"), wide, wide,
            spread, spread, spread, wide, wide, wide, spread, spread, spread,
        ),
        check_vma=False,
    )
```

profile of v0, /device:TPU:0, one launch (start us, length us, event | category | flops | bytes accessed | tf_op | source)
XLA Modules:
  0.0 345.9 jit_solution(1691346540914008487)
XLA Ops:
  0.6 0.0 copy-start
  0.7 0.0 copy-start.2
  0.7 0.0 copy-start.3
  0.7 0.0 copy-start.10
  0.7 0.8 broadcast_add_fusion
  1.5 0.6 dynamic_slice.18.live
  2.0 1.1 copy.37
  3.1 0.0 copy-start.4
  3.1 0.0 copy-start.5
  3.1 0.0 copy-start.6
  3.2 0.0 copy-start.7
  3.2 0.0 copy-start.8
  3.2 0.0 copy-start.9
  3.2 2.0 pad_maximum_fusion.shard
  5.2 0.7 tile.20
  5.9 0.1 tile.21
  6.0 0.1 broadcast_in_dim.52
  6.1 0.7 tile.8
  6.8 0.1 tile.9
  6.9 0.1 pad.3.clone
  7.0 0.7 maximum_bitcast_fusion.small
  7.7 0.0 copy-done.10
  7.7 0.1 select_reduce_fusion
  7.8 0.0 copy-done
  7.8 0.0 copy-done.2
  7.8 0.0 copy-done.3
  7.8 1.5 add_convert_fusion.h
  9.3 0.9 broadcast_in_dim.57.fraction
  10.2 0.0 copy-done.4
  10.2 0.0 copy-done.5
  10.2 0.0 copy-done.6
  10.2 0.0 copy-done.7
  10.2 0.0 copy-done.8
  10.2 0.0 copy-done.9
  10.2 0.7 stack.29.vecs
  10.9 155.2 %forward.1 = (bf16[4,4,256,1024]{3,2,1,0:T(8,128)(2,1)}, bf16[4,4,256,1024]{3,2,1,0:T(8,128)(2,1)}, bf16[4,4,256,1024]{3,2,1,0:T(8,128)(2,1)}, bf16[4,16,1024]{2...) custom-call(s32[2]{0:T(128)} %dynamic_slice.18.live, ...), custom_call_target="tpu_custom_call" | custom-call | tf_op jit(solution)/shard_map/forward/pallas_call | solution.py:476
  166.1 0.6 dynamic_slice.19.portion
  166.7 165.0 %backward.1 = (f32[12,256,128]{2,1,0:T(8,128)}, f32[16,1024]{1,0:T(8,128)}, f32[640,1024]{1,0:T(8,128)}, bf16[12,4,256,1024]{3,2,1,0:T(8,128)(2,1)}) custom-call(s32[2]{0:T(128)} %dynamic_slice.18.live, f32[2]{0:T(128)} %dynamic_slice.19.portion, bf16[4,4,256,1024]{3,2,1,0:T(8,128)(2,1)} %get-tuple-element.38.w_one, ...), custom_call_target="tpu_custom_call" | custom-call | tf_op jit(solution)/shard_map/backward/pallas_call | solution.py:999
  331.7 0.7 constant_dynamic-slice_fusion.2
  332.5 0.5 slice_bitcast_fusion.2
  333.0 1.0 slice_bitcast_fusion
  334.0 0.9 copy.39
  335.0 0.8 slice.46
  335.7 0.1 reshape.97
  335.8 0.1 reshape.98
  335.9 0.7 dynamic_slice.21
  336.6 1.6 slice_bitcast_fusion.1
  338.1 0.0 copy-start.1
  338.1 2.4 fusion.3
  340.5 0.7 constant_dynamic-slice_fusion
  341.2 0.7 constant_dynamic-slice_fusion.1
  341.9 2.5 copy.42
  344.4 0.0 copy-done.1
  344.4 1.5 copy.43
  (11 shorter events, 0.1 us)
Async XLA Ops:
  0.6 7.1 %copy-start = (bf16[640,1024]{1,0:T(8,128)(2,1)S(1)}, bf16[640,1024]{1,0:T(8,128)(2,1)}, u32[]{:S(2)}) copy-start(bf16[640,1024]{1,0:T(8,128)(2,1)} %tokens.1) | copy-start | bytes 3932164
  0.7 7.1 %copy-start.2 = (f32[1024]{0:T(1024)S(1)}, f32[1024]{0:T(1024)}, u32[]{:S(2)}) copy-start(f32[1024]{0:T(1024)} %param.22) | copy-start | bytes 12292
  0.7 7.1 %copy-start.3 = (f32[1024]{0:T(1024)S(1)}, f32[1024]{0:T(1024)}, u32[]{:S(2)}) copy-start(f32[1024]{0:T(1024)} %param.21) | copy-start | bytes 12292
  0.7 7.0 %copy-start.10 = (s32[5]{0:T(128)S(1)}, s32[5]{0:T(128)}, u32[]{:S(2)}) copy-start(s32[5]{0:T(128)} %param.20) | copy-start | bytes 64
  3.1 7.1 %copy-start.4 = (f32[1024]{0:T(1024)S(1)}, f32[1024]{0:T(1024)}, u32[]{:S(2)}) copy-start(f32[1024]{0:T(1024)} %param.26) | copy-start | bytes 12292
  3.1 7.1 %copy-start.5 = (f32[1024]{0:T(1024)S(1)}, f32[1024]{0:T(1024)}, u32[]{:S(2)}) copy-start(f32[1024]{0:T(1024)} %param.27) | copy-start | bytes 12292
  3.1 7.1 %copy-start.6 = (f32[1024]{0:T(1024)S(1)}, f32[1024]{0:T(1024)}, u32[]{:S(2)}) copy-start(f32[1024]{0:T(1024)} %param.28) | copy-start | bytes 12292
  3.2 7.0 %copy-start.7 = (f32[1024]{0:T(1024)S(1)}, f32[1024]{0:T(1024)}, u32[]{:S(2)}) copy-start(f32[1024]{0:T(1024)} %param.32) | copy-start | bytes 12292
  3.2 7.0 %copy-start.8 = (f32[1024]{0:T(1024)S(1)}, f32[1024]{0:T(1024)}, u32[]{:S(2)}) copy-start(f32[1024]{0:T(1024)} %param.33) | copy-start | bytes 12292
  3.2 7.0 %copy-start.9 = (f32[1024]{0:T(1024)S(1)}, f32[1024]{0:T(1024)}, u32[]{:S(2)}) copy-start(f32[1024]{0:T(1024)} %param.34) | copy-start | bytes 12292
  338.1 6.2 %copy-start.1 = (f32[640,1024]{1,0:T(8,128)S(1)}, f32[640,1024]{1,0:T(8,128)}, u32[]{:S(2)}) copy-start(f32[640,1024]{1,0:T(8,128)} %get-tuple-element.119) | copy-start | bytes 7864324
where the time goes:
time: 347 us; the launch traced here: 346 us
  Pallas kernels  320 us (92%)
  local copies, waits for them, and re-layouts  19.7 us (6%)
  other arithmetic  5.09 us (1%)
    pallas_call x1, Pallas kernels, backward_pass(): pl.pallas_call(functools.partial(backward_kernel, outer), out_shape=(jax....  165 us
    pallas_call x1, Pallas kernels, forward_pass(): pl.pallas_call(functools.partial(forward_kernel, outer), out_shape=(weigh...  155 us

commit v1 on v0

--- a/solution.py
+++ b/solution.py
@@ -17,6 +17,7 @@
 F32 = jnp.float32
 PIECES = 12
 LANES = 4
+PARTS = 5
 ROWS = 256
 COLS = 128
 VMEM_LIMIT = 62 * 2**20
@@ -92,6 +93,11 @@
     return pl.ds(pl.multiple_of(lane * COLS, COLS), COLS)
 
 
+def load_lanes(src, dst, sem):
+    for lane in range(8):
+        pltpu.make_async_copy(src.at[lane], dst.at[:, :, lane * COLS : (lane + 1) * COLS], sem).start()
+
+
 def tile_rows(start, size):
     return pl.ds(pl.multiple_of(start, 128), size)
 
@@ -116,7 +122,7 @@
 
 
 def forward_kernel(
-    outer, live, shard, small, h, tokens, cotangent, fraction, vecs,
+    outer, context, timestep, shard_one, shard_up, shard_down, small, h, tokens, cotangent, vecs,
     w_one, w_up, w_down, small_full, h_win_out, q_out, k_out, v_out, attn_out, y_out, hidden_out, slope_out,
     xhat_out, dz_out, grad_f_out, layer_out, lse, rstd_out, sums,
     h_win, q, k, v, attn, y_low, hidden, slope, xhat, acc, pre, grad_f, out_rows, bias_in, bias, wbuf, v_t,
@@ -129,11 +135,15 @@
     groups = (w_one, w_up, w_down)
     x_lane, y_lane, d_lane = at.side * 2 + at.core, at.over * 2 + at.core, at.diag * 2 + at.core
 
-    def source(p):
-        return small if p is None else shard.at[pl.ds(p, 1)]
+    shards = (shard_one, shard_up, shard_down)
 
     def block(ref, lane, start, count):
-        return ref.at[pl.ds(start, count), :, cols_of(lane)]
+        if ref is small_full:
+            return ref.at[pl.ds(start, count), :, cols_of(lane)]
+        return ref.at[lane, pl.ds(start, count)]
+
+    def some(ref, lanes):
+        return ref.at[:, :, 0 : lanes * COLS] if ref is small_full else ref.at[0:lanes]
 
     def index(p):
         return PIECES if p is None else p
@@ -141,27 +151,27 @@
     def grouped(action):
         def run(p):
             if p is None:
-                action(None, small_full)
+                action(None, small_full, small)
                 return
             if isinstance(p, int):
-                action(p, groups[p // 4].at[p % 4])
+                action(p, groups[p // 4].at[p % 4], shards[p // 4].at[pl.ds(p % 4, 1)])
                 return
             for g, ref in enumerate(groups):
                 @pl.when(lax.div(p, 4) == g)
                 def _():
-                    action(p, ref.at[p - 4 * g])
+                    action(p, ref.at[p - 4 * g], shards[g].at[pl.ds(p - 4 * g, 1)])
 
         return run
 
-    def first(p, ref):
-        i, src, dst = index(p), source(p), block(ref, at.own, z, 1)
+    def first(p, ref, src):
+        i, dst = index(p), block(ref, at.own, z, 1)
         send(src, dst, sent.at[i], got_x.at[i], at.beside())
         send(src, dst, sent.at[i], got_y.at[i], at.across())
         for step_z in range(1, 4):
             send(src, dst, sent.at[i], got_z.at[i], at.along(step_z))
         send(src, dst, sent.at[i], got_c.at[i], at.partner())
 
-    def second(p, ref):
+    def second(p, ref, _):
         i = index(p)
         wait_for(block(ref, at.own, 0, 3), got_z.at[i])
         for step_z in range(1, 4):
@@ -170,7 +180,7 @@
             send(part, part, sent.at[i], got_y.at[i], at.across())
             send(part, part, sent.at[i], got_c.at[i], at.partner())
 
-    def third(p, ref):
+    def third(p, ref, _):
         i = index(p)
         wait_for(block(ref, x_lane, 0, 4), got_x.at[i])
         part = block(ref, x_lane, 0, 2)
@@ -183,48 +193,46 @@
         part = block(ref, y_lane, 0, 4)
         send(part, part, sent.at[i], got_c.at[i], at.partner())
 
-    def fourth(p, ref):
+    def fourth(p, ref, _):
         i = index(p)
         wait_for(block(ref, d_lane, 0, 2), got_yd.at[i])
         wait_for(block(ref, d_lane, 2, 2), got_xd.at[i])
         part = block(ref, d_lane, 0, 4)
         send(part, part, sent.at[i], got_c.at[i], at.partner())
 
-    def load(p, ref):
-        slot = lax.rem(p, 3)
-        return pltpu.make_async_copy(ref, wbuf.at[slot], load_sem.at[slot])
-
-    def fifth(p, ref):
-        wait_for(ref.at[:, :, 0 : 4 * COLS], got_c.at[index(p)])
+    def fifth(p, ref, _):
+        wait_for(some(ref, 4), got_c.at[index(p)])
         if p is None:
             pltpu.make_async_copy(small_full, bias_in, own_sem.at[1]).start()
         else:
-            load(p, ref).start()
-
-    def drain(p, ref):
-        wait_for(ref.at[:, :, 0 : 7 * COLS], sent.at[index(p)])
-        wait_for(ref.at[0:3, :, 0:COLS], sent.at[index(p)])
+            load_lanes(ref, wbuf.at[lax.rem(p, 3)], load_sem.at[lax.rem(p, 3)])
+
+    def drain(p, ref, _):
+        wait_for(some(ref, 7), sent.at[index(p)])
+        wait_for(block(ref, 0, 0, 3), sent.at[index(p)])
 
     first, second, third, fourth, fifth, drain = (
         grouped(action) for action in (first, second, third, fourth, fifth, drain)
     )
 
-    def halo():
-        for i in range(3):
-            @pl.when(jnp.logical_and(z >= 1, z < 4 - i))
-            def _():
-                dst = h_win.at[tile_rows((4 + z + i) * step, step)]
-                send(h.at[tile_rows(i * step, step)], dst, halo_sent, halo_got, at.along(3))
-
-            @pl.when(jnp.logical_and(z <= 2, z >= i))
-            def _():
-                dst = h_win.at[tile_rows(i * step, step)]
-                send(h.at[tile_rows((4 - z + i) * step, step)], dst, halo_sent, halo_got, at.along(1))
+    def halo(part):
+        i, small_step = part // 2, step // 2
+
+        def some_rows(start):
+            first_row = start * step + part % 2 * small_step
+            return pl.ds(pl.multiple_of(first_row, small_step), small_step)
+
+        @pl.when(jnp.logical_and(z >= 1, z < 4 - i))
+        def _():
+            dst = h_win.at[some_rows(4 + z + i)]
+            send(h.at[some_rows(i)], dst, halo_sent, halo_got, at.along(3))
+
+        @pl.when(jnp.logical_and(z <= 2, z >= i))
+        def _():
+            send(h.at[some_rows(4 - z + i)], h_win.at[some_rows(i)], halo_sent, halo_got, at.along(1))
 
     mine = [
-        pltpu.make_async_copy(
-            shard.at[4 * g : 4 * g + 4], ref.at[:, z, :, cols_of(at.own)], own_sem.at[2 + g]
-        )
+        pltpu.make_async_copy(shards[g], ref.at[:, at.own, z], own_sem.at[2 + g])
         for g, ref in enumerate(groups)
     ] + [pltpu.make_async_copy(small, small_full.at[pl.ds(z, 1), :, cols_of(at.own)], own_sem.at[0])]
     stores = []
@@ -244,7 +252,7 @@
 
     def weight(p):
         slot = lax.rem(p, 3)
-        pltpu.make_async_copy(w_one.at[0], wbuf.at[slot], load_sem.at[slot]).wait()
+        wait_for(wbuf.at[slot], load_sem.at[slot])
         return slot
 
     def make_bias():
@@ -292,7 +300,7 @@
                 span = tile_rows(slot * 4 * step, 4 * step)
                 here = slice(j * step, (j + 1) * step)
                 q_two = split_heads(q[here, lanes] * jnp.asarray(0.125, BF))
-                scores = masked_scores(k[span, lanes], q_two, jnp.where(slot == 0, live[0], live[1]))
+                scores = masked_scores(k[span, lanes], q_two, context[z + slot] + BLOCK)
                 row_max = jnp.max(scores, axis=0, keepdims=True)
                 expo = jnp.exp(scores - row_max)
                 total = jnp.sum(expo, axis=0, keepdims=True)
@@ -320,14 +328,19 @@
         tiles(one)
         store(attn, attn_out)
 
-        def norm(here):
-            h_zero = tokens[here, :].astype(F32) + fraction[here, 0:1] * vecs[0:1, :] + vecs[1:2, :]
+        def norm(here, i):
+            share = timestep[z + lax.div(z + lax.div(i * 32, step), 4)].astype(F32) * (1.0 / TSTEPS)
+            h_zero = tokens[here, :].astype(F32) + share * vecs[0:1, :] + vecs[1:2, :]
             normal, rstd = norm_rows(h_zero + acc[here, :] + vecs[2:3, :])
             xhat[here, :] = normal
             y_low[here, :] = (normal * vecs[3:4, :] + vecs[4:5, :]).astype(BF)
             rstd_out[here, :] = jnp.broadcast_to(rstd, (rstd.shape[0], COLS))
 
-        row_loop(32, norm)
+        def run(i, carry):
+            norm(pl.ds(pl.multiple_of(i * 32, 32), 32), i)
+            return carry
+
+        lax.fori_loop(0, rows // 32, run, 0)
         acc[...] = jnp.zeros_like(acc)
         store(y_low, y_out)
         store(xhat, xhat_out)
@@ -397,7 +410,6 @@
     first(None)
     first(0)
     first(1)
-    halo()
     for copy in mine:
         copy.start()
     stages = ((second, 0), (third, -1), (fourth, -2), (fifth, -3))
@@ -421,6 +433,10 @@
             @pl.when(t == -shift)
             def _():
                 action(None)
+        for part in range(6):
+            @pl.when(t == min(part, 4))
+            def _():
+                halo(part)
         for when, actions in work.items():
             @pl.when(t == when)
             def _():
@@ -431,13 +447,11 @@
         def _():
             up_piece(t - 5)
 
-        @pl.when(t >= 13)
-        def _():
-            down_piece(t - 5)
-
+        for i in range(2):
+            when_in(2 * (t - 13) + i - 1, 4, lambda n: down_piece(n + 8))
         return carry
 
-    lax.fori_loop(0, PIECES + 5, tick, 0)
+    lax.fori_loop(0, PIECES + 4, tick, 0)
     finish()
     middle = jnp.logical_and(z >= 1, z <= 2)
 
@@ -463,11 +477,11 @@
         pltpu.make_async_copy(src, dst, store_sem.at[i]).wait()
 
 
-def forward_pass(outer, live, shard, small, h, tokens, cotangent, fraction, vecs):
+def forward_pass(outer, context, timestep, *arrays):
     sem = pltpu.SemaphoreType.DMA
-    rows, model = h.shape
+    rows, model = arrays[4].shape
     win = rows // 5 * 8
-    weights = jax.ShapeDtypeStruct((4, 4, ROWS, model), BF)
+    weights = jax.ShapeDtypeStruct((4, 8, 4, ROWS, COLS), BF)
     own = jax.ShapeDtypeStruct((rows, model), BF)
     own_wide = jax.ShapeDtypeStruct((rows, model), F32)
     window = jax.ShapeDtypeStruct((win, model), BF)
@@ -482,7 +496,7 @@
             jax.ShapeDtypeStruct((rows, COLS), F32),
             jax.ShapeDtypeStruct((3, 8, model), F32),
         ),
-        in_specs=[pl.BlockSpec(memory_space=pltpu.SMEM)] + [vmem] * 7,
+        in_specs=[pl.BlockSpec(memory_space=pltpu.SMEM)] * 2 + [vmem] * 8,
         out_specs=[anywhere] * 16 + [vmem] * 3,
         scratch_shapes=[
             pltpu.VMEM((win, model), BF),
@@ -510,7 +524,7 @@
             collective_id=1, has_side_effects=True, vmem_limit_bytes=VMEM_LIMIT
         ),
         name="forward",
-    )(live, shard, small, h, tokens, cotangent, fraction, vecs)
+    )(context, timestep, *arrays)
 
 
 def split_heads(rows):
@@ -531,14 +545,14 @@
 
 
 def backward_kernel(
-    outer, live, portion, w_one, w_up, w_down, h_win_in, q_in, k_in, v_in, attn_in, y_in, hidden_in, slope_in,
+    outer, context, timestep, w_one, w_up, w_down, h_win_in, q_in, k_in, v_in, attn_in, y_in, hidden_in, slope_in,
     xhat_in, dz_in, grad_f_in, lse, rstd, vecs, sums_in,
-    out, sums_out, tokens_out, pieces,
+    out_down, out_up, out_one, out_qkv, sums_out, tokens_out,
     part, lane, got_c, got_dx, got_dy, got_x, got_y, got_z,
-    wbuf, hidden, slope, y_low, grad_f, acc, xhat, attn, q, k, v, h_win, dk_acc, dv_acc, k_t, dh_low, halo_in,
-    dtile, wide_tile, stage, stats, s_sum, s_got,
-    part_sem, sent0, sent1, sent2, sent3, sem_c, sem_dx, sem_dy, sem_x, sem_y, sem_z,
-    in_sem, hidden_sem, weight_sem, stage_sem, token_sem, halo_sent, halo_got, small_sent, small_got, credit,
+    wbuf, hidden, slope, y_low, grad_f, acc, xhat, attn, q, k, v, h_win, dk_acc, dv_acc, k_t, halo_in,
+    dtile, wide_tile, stats, s_sum, s_got,
+    sent0, sent1, sent2, sent3, sem_c, sem_dx, sem_dy, sem_x, sem_y, sem_z,
+    in_sem, hidden_sem, weight_sem, token_sem, halo_sent, halo_got, small_sent, small_got, credit,
 ):
     at = Place(outer)
     greet(at)
@@ -563,29 +577,27 @@
         )
 
     def get_weight(ref, slot):
-        return pltpu.make_async_copy(ref, wbuf.at[slot], weight_sem.at[slot])
-
-    def put_piece(p):
-        return pltpu.make_async_copy(stage, pieces.at[p], stage_sem)
-
-    def get_part(p):
-        slot = lax.rem(p, 2)
-        return pltpu.make_async_copy(pieces.at[p], part.at[slot], part_sem.at[slot])
+        load_lanes(ref, wbuf.at[slot], weight_sem.at[slot])
+
+    def have_weight(slot):
+        wait_for(wbuf.at[slot], weight_sem.at[slot])
+
+    def share(slot):
+        return timestep[z + slot].astype(F32) * (1.0 / TSTEPS)
 
     def first(p):
-        slot = lax.rem(p, 2)
-        get_part(p).wait()
+        slot, src_slot = lax.rem(p, 2), lax.rem(p, PARTS)
 
         @pl.when(p >= 2)
         def _():
             pl.semaphore_wait(credit, 1)
 
         for a in range(4):
-            src = part.at[slot, :, :, cols_of(a * 2 + 1 - at.core)]
+            src = part.at[src_slot, :, :, cols_of(a * 2 + 1 - at.core)]
             send(src, got_c.at[slot, a], sent0.at[p], sem_c.at[p], at.partner())
 
     def second(p):
-        slot, row = lax.rem(p, 2), lax.rem(p, LANES)
+        slot, row, src_slot = lax.rem(p, 2), lax.rem(p, LANES), lax.rem(p, PARTS)
         wait_for(got_c.at[slot], sem_c.at[p])
 
         @pl.when(p >= LANES)
@@ -596,7 +608,7 @@
 
         def add(i, carry):
             a, b = lax.div(i, 4), lax.rem(i, 4)
-            lane[row, a, b] = part[slot, b, :, cols_of(a * 2 + at.core)] + got_c[slot, a, b]
+            lane[row, a, b] = part[src_slot, b, :, cols_of(a * 2 + at.core)] + got_c[slot, a, b]
             return carry
 
         lax.fori_loop(0, 16, add, 0)
@@ -650,17 +662,22 @@
         for far in range(3):
             total = total + got_z[p, far].astype(F32)
 
-        @pl.when(p < 8)
-        def _():
-            out[lax.rem(p, 2) * 4 + lax.div(p, 2)] = total
+
+        @pl.when(jnp.logical_and(p < 8, lax.rem(p, 2) == 0))
+        def _():
+            out_down[lax.rem(lax.div(p, 2), 4)] = total
+
+        @pl.when(jnp.logical_and(p < 8, lax.rem(p, 2) == 1))
+        def _():
+            out_up[lax.rem(lax.div(p, 2), 4)] = total
 
         @pl.when(p == 8)
         def _():
-            out[8] = total
+            out_one[...] = total
 
         @pl.when(p > 8)
         def _():
-            out[20 - p] = total
+            out_qkv[11 - p] = total.T
 
     def tiles(action):
         def run(n, carry):
@@ -677,11 +694,12 @@
         lax.fori_loop(0, rows // count, run, 0)
 
     def produce(p, left, right):
+        slot = lax.rem(p, PARTS)
+
         def one(n, span):
-            stage[n] = dot_tn(left[:, span], right()).astype(BF)
+            part[slot, n] = dot_tn(left[:, span], right()).astype(BF)
 
         tiles(one)
-        put_piece(p).start()
 
     def grad_down(i):
         @pl.when(i == 0)
@@ -691,15 +709,11 @@
         for copy in get_hidden(i):
             copy.wait()
 
-        @pl.when(i > 0)
-        def _():
-            put_piece(2 * i - 1).wait()
-
         produce(2 * i, hidden.at[lax.rem(i, 2)], lambda: grad_f[...])
 
     def grad_pre(i):
         slot = lax.rem(i, 2)
-        get_weight(w_down.at[i], 0).wait()
+        have_weight(0)
 
         def one(n, span):
             dtile[...] = dot_nt(grad_f[...], wbuf[0, n])
@@ -716,23 +730,22 @@
 
         @pl.when(i < 3)
         def _():
-            get_weight(w_down.at[lax.rem(i + 1, 4)], 0).start()
+            get_weight(w_down.at[lax.rem(i + 1, 4)], 0)
 
         @pl.when(i == 3)
         def _():
-            get_weight(w_one.at[3], 0).start()
+            get_weight(w_one.at[3], 0)
 
     def grad_up(i):
         @pl.when(i == 0)
         def _():
             get(1).wait()
 
-        put_piece(2 * i).wait()
         produce(2 * i + 1, slope.at[lax.rem(i, 2)], lambda: y_low[...])
 
     def grad_y(i):
         slot = lax.rem(i, 2)
-        get_weight(w_up.at[i], 1).wait()
+        have_weight(1)
 
         @pl.when(i == 0)
         def _():
@@ -746,11 +759,11 @@
 
         @pl.when(i < 3)
         def _():
-            get_weight(w_up.at[lax.rem(i + 1, 4)], 1).start()
+            get_weight(w_up.at[lax.rem(i + 1, 4)], 1)
 
         @pl.when(i == 3)
         def _():
-            get_weight(w_one.at[1], 1).start()
+            get_weight(w_one.at[1], 1)
 
         @pl.when(i < 2)
         def _():
@@ -782,16 +795,16 @@
             stats[2] += fold_rows(low.astype(F32))
 
         row_loop(32, back)
-        put_piece(7).wait()
+
+    def grad_out():
         produce(8, attn, lambda: grad_f[...])
-        get_weight(w_one.at[3], 0).wait()
+        have_weight(0)
 
         def one(n, span):
             y_low[:, span] = dot_nt(grad_f[...], wbuf[0, n]).astype(BF)
 
         tiles(one)
-        get_weight(w_one.at[2], 0).start()
-        put_piece(8).wait()
+        get_weight(w_one.at[2], 0)
         for i in range(5, 9):
             get(i).wait()
 
@@ -808,7 +821,7 @@
                 here = slice(j * step, (j + 1) * step)
                 q_two = split_heads(q[here, lanes] * jnp.asarray(0.125, BF))
                 g_two = split_heads(y_low[here, lanes])
-                scores = masked_scores(k[span, lanes], q_two, jnp.where(slot == 0, live[0], live[1]))
+                scores = masked_scores(k[span, lanes], q_two, context[z + slot] + BLOCK)
                 probs = jnp.exp(scores - lse[i, j : j + 1, :])
                 dv_acc[span, :] += dot_nn(probs.astype(BF), g_two)
                 grad_p = dot_nt(v[span, lanes], g_two)
@@ -829,49 +842,43 @@
 
     def grad_value():
         produce(9, v, lambda: h_win[...])
-        put_piece(9).wait()
 
     def grad_key_query():
         produce(10, k, lambda: h_win[...])
-        put_piece(10).wait()
         produce(11, q, lambda: h_win[tile_rows(z * step, rows), :])
 
-    def share(slot):
-        return jnp.where(slot == 0, portion[0], portion[1])
-
     def input_window():
-        get_weight(w_one.at[1], 1).wait()
-        get_weight(w_one.at[2], 0).wait()
+        have_weight(1)
+        have_weight(0)
 
         def one(n, span):
             wide_k = wbuf[1, :, :, span].reshape(model, ROWS)
             wide_v = wbuf[0, :, :, span].reshape(model, ROWS)
             wide_tile[...] = dot_nn(k[...], wide_k) + dot_nn(v[...], wide_v)
-            dh_low[:, span] = wide_tile[...].astype(BF)
+            h_win[:, span] = wide_tile[...].astype(BF)
             low = fold_rows(wide_tile[0 : 4 * step, :])
             high = fold_rows(wide_tile[4 * step : 8 * step, :])
-            stats[0, :, span] = low * portion[0] + high * portion[1]
+            stats[0, :, span] = low * share(0) + high * share(1)
             stats[1, :, span] = low + high
 
         tiles(one)
-        get_weight(w_one.at[0], 1).start()
-        put_piece(11).wait()
+        get_weight(w_one.at[0], 1)
 
         for i in range(3):
             @pl.when(z > i)
             def _():
-                src = dh_low.at[tile_rows(i * step, step)]
+                src = h_win.at[tile_rows(i * step, step)]
                 dst = halo_in.at[tile_rows((5 - z + i) * step, step)]
                 send(src, dst, halo_sent, halo_got, at.along(3))
 
             @pl.when(z < 3 - i)
             def _():
-                src = dh_low.at[tile_rows((5 + z + i) * step, step)]
+                src = h_win.at[tile_rows((5 + z + i) * step, step)]
                 dst = halo_in.at[tile_rows(i * step, step)]
                 send(src, dst, halo_sent, halo_got, at.along(1))
 
     def input_own():
-        get_weight(w_one.at[0], 1).wait()
+        have_weight(1)
 
         def one(n, span):
             acc[:, span] += dot_nn(q[...], wbuf[1, :, :, span].reshape(model, ROWS))
@@ -917,7 +924,7 @@
 
         for j in range(5):
             block = slice(j * step, (j + 1) * step)
-            acc[block, :] += dh_low[tile_rows((z + j) * step, step), :].astype(F32)
+            acc[block, :] += h_win[tile_rows((z + j) * step, step), :].astype(F32)
             upper = jnp.logical_and(z <= 2, j >= 4 - z)
             lower = jnp.logical_and(z >= 1, j < 4 - z)
 
@@ -931,18 +938,18 @@
     for i in range(2):
         for copy in get_hidden(i):
             copy.start()
-    get_weight(w_down.at[0], 0).start()
+    get_weight(w_down.at[0], 0)
     for i in range(1, 3):
         get(i).start()
-    get_weight(w_up.at[0], 1).start()
+    get_weight(w_up.at[0], 1)
     for i in range(3, 9):
         get(i).start()
     work = {
         5: (norm_one,),
-        6: (lambda: attend_pairs(0, 2),),
-        7: (lambda: attend_pairs(2, 2),),
-        8: (lambda: attend_pairs(4, 2),),
-        9: (lambda: attend_pairs(6, 2), grad_value),
+        6: (grad_out, lambda: attend_pairs(0, 1)),
+        7: (lambda: attend_pairs(1, 3),),
+        8: (lambda: attend_pairs(4, 3),),
+        9: (lambda: attend_pairs(7, 1), grad_value),
         10: (grad_key_query,),
         11: (input_window,),
         12: (input_own, lambda: small_send(0)),
@@ -953,17 +960,14 @@
 
     def slot_run(s, carry):
         c = s - 1
-        when_in(c, PIECES, lambda p: get_part(p).start())
         for action, shift in ((second, 1), (third, 2), (fourth, 3), (fifth, 4), (first, 0)):
             when_in(c - shift, PIECES, action)
 
-        @pl.when(s < 6)
-        def _():
-            def sub_step(u, inner):
-                when_in(3 * s + u, 16, feed_forward)
-                return inner
-
-            lax.fori_loop(0, 3, sub_step, 0)
+        def sub_step(u, inner):
+            when_in(3 * s - 2 + u, 16, feed_forward)
+            return inner
+
+        lax.fori_loop(0, 3, sub_step, 0)
 
         for when, actions in work.items():
             @pl.when(s == when)
@@ -984,12 +988,12 @@
     for i in range(3):
         wait_for(s_sum.at[i], small_sent.at[i])
     wait_for(s_got.at[0:3], small_sent.at[3])
-    wait_for(dh_low.at[0 : 3 * step], halo_sent)
+    wait_for(h_win.at[0 : 3 * step], halo_sent)
     for j in range(5):
         put_tokens(j).wait()
 
 
-def backward_pass(outer, live, portion, *arrays):
+def backward_pass(outer, context, timestep, *arrays):
     sem = pltpu.SemaphoreType.DMA
     model = 8 * COLS
     rows = arrays[4].shape[0]
@@ -999,15 +1003,17 @@
     return pl.pallas_call(
         functools.partial(backward_kernel, outer),
         out_shape=(
-            jax.ShapeDtypeStruct((PIECES, ROWS, COLS), F32),
+            jax.ShapeDtypeStruct((4, ROWS, COLS), F32),
+            jax.ShapeDtypeStruct((4, ROWS, COLS), F32),
+            jax.ShapeDtypeStruct((ROWS, COLS), F32),
+            jax.ShapeDtypeStruct((3, COLS, ROWS), F32),
             jax.ShapeDtypeStruct((16, model), F32),
             jax.ShapeDtypeStruct((rows, model), F32),
-            jax.ShapeDtypeStruct((PIECES, 4, ROWS, model), BF),
         ),
         in_specs=[pl.BlockSpec(memory_space=pltpu.SMEM)] * 2 + [anywhere] * 14 + [vmem] * 4,
-        out_specs=[vmem, vmem, anywhere, anywhere],
+        out_specs=[vmem] * 5 + [anywhere],
         scratch_shapes=[
-            pltpu.VMEM((2, 4, ROWS, model), BF),
+            pltpu.VMEM((PARTS, 4, ROWS, model), BF),
             pltpu.VMEM((LANES,) + half, BF),
             pltpu.VMEM((2,) + half, BF),
             pltpu.VMEM((PIECES, 2, ROWS, COLS), BF),
@@ -1030,26 +1036,23 @@
             pltpu.VMEM((win, COLS), F32),
             pltpu.VMEM((win, COLS), F32),
             pltpu.VMEM((COLS, win), BF),
-            pltpu.VMEM((win, model), BF),
             pltpu.VMEM((rows, model), BF),
             pltpu.VMEM((rows, ROWS), F32),
             pltpu.VMEM((win, ROWS), F32),
-            pltpu.VMEM((4, ROWS, model), BF),
             pltpu.VMEM((14, 8, model), F32),
             pltpu.VMEM((4, 16, model), F32),
             pltpu.VMEM((6, 16, model), F32),
-            sem((2,)),
         ]
         + [sem((PIECES,))] * 10
         + [
-            sem((9,)), sem((4,)), sem((2,)), sem, sem((5,)), sem, sem, sem((4,)), sem((4,)),
+            sem((9,)), sem((4,)), sem((2,)), sem((5,)), sem, sem, sem((4,)), sem((4,)),
             pltpu.SemaphoreType.REGULAR,
         ],
         compiler_params=pltpu.CompilerParams(
             collective_id=2, has_side_effects=True, vmem_limit_bytes=VMEM_LIMIT
         ),
         name="backward",
-    )(live, portion, *arrays)
+    )(context, timestep, *arrays)
 
 
 def body(
@@ -1068,14 +1071,8 @@
             lax.all_gather(w, "dp", axis=1, tiled=True, axis_index_groups=groups)
             for w in (qkv_weight, out_weight, up_weight, down_weight, qv_bias, up_bias)
         )
-    shard = jnp.concatenate(
-        [
-            qkv_weight.transpose(0, 2, 1),
-            out_weight.reshape(1, ROWS, COLS),
-            up_weight.reshape(4, ROWS, COLS),
-            down_weight.reshape(4, ROWS, COLS),
-        ]
-    )
+    shard_one = jnp.concatenate([qkv_weight.transpose(0, 2, 1), out_weight.reshape(1, ROWS, COLS)])
+    shard_up, shard_down = (w.reshape(4, ROWS, COLS) for w in (up_weight, down_weight))
     own = lax.div(lax.axis_index("dp"), outer)
     n_up, n_qv = up_bias.size, qv_bias.size
     part = jnp.arange(COLS) // up_bias.shape[1]
@@ -1089,7 +1086,6 @@
     portion = timestep.astype(F32) / TSTEPS
     fraction = jnp.sum(jnp.where(owner, portion[None, :], 0.0), axis=1)
     h_low = (tokens.astype(F32) + fraction[:, None] * time_weight + time_bias).astype(BF)
-    live = lax.dynamic_slice((context + BLOCK).astype(jnp.int32), (z,), (2,))
     vecs = jnp.stack(
         [time_weight, time_bias, out_bias, gain_one, shift_one, down_bias, gain_two, shift_two]
     )
@@ -1097,16 +1093,14 @@
         w_one, w_up, w_down, _, h_win, queries, keys, values, attn, y_low, hidden, slope, xhat, grad_z2,
         grad_f, layer_out, lse, rstd, sums,
     ) = forward_pass(
-        outer, live, shard, small, h_low, tokens, cotangent,
-        jnp.broadcast_to(fraction[:, None], (rows, COLS)), vecs,
+        outer, context, timestep, shard_one, shard_up, shard_down, small, h_low, tokens, cotangent, vecs,
     )
-    done, totals, grad_tokens, _ = backward_pass(
-        outer, live, lax.dynamic_slice(portion, (z,), (2,)), w_one, w_up, w_down, h_win, queries, keys,
+    grad_down, grad_up, grad_out_w, grad_qkv, totals, grad_tokens = backward_pass(
+        outer, context, timestep, w_one, w_up, w_down, h_win, queries, keys,
         values, attn, y_low, hidden, slope, xhat, grad_z2, grad_f, lse, rstd, vecs, sums,
     )
     weight_grads = [
-        done[9:12].transpose(0, 2, 1), done[8], done[4:8].reshape(4 * ROWS, COLS),
-        done[0:4].reshape(4 * ROWS, COLS),
+        grad_qkv, grad_out_w, grad_up.reshape(4 * ROWS, COLS), grad_down.reshape(4 * ROWS, COLS)
     ]
     if outer > 1:
         weight_grads = [

time: 347 us -> 321 us (0.925)
  Pallas kernels: 320 us -> 299 us
  local copies, waits for them, and re-layouts: 19.7 us -> 14.9 us
    pallas_call x1, Pallas kernels: 155 us -> 143 us  [forward_pass(): pl.pallas_call(functools.partial(forward_kernel, outer), out_shape=(weigh...]
    pallas_call x1, Pallas kernels: 165 us -> 156 us  [backward_pass(): pl.pallas_call(functools.partial(backward_kernel, outer), out_shape=(jax....]
    unnamed x26 -> x33, local copies, waits for them, and re-layouts: 6.02 us -> 8.13 us
where the time goes in v1:
time: 321 us
  Pallas kernels  299 us (93%)
  local copies, waits for them, and re-layouts  14.9 us (5%)
  other arithmetic  5.87 us (2%)
    pallas_call x1, Pallas kernels, backward_pass(): pl.pallas_call(functools.partial(backward_kernel, outer), out_shape=(jax....  156 us
    pallas_call x1, Pallas kernels, forward_pass(): pl.pallas_call(functools.partial(forward_kernel, outer), out_shape=(weigh...  143 us
    unnamed x33, local copies, waits for them, and re-layouts  8.13 us

profile of v1, /device:TPU:0, one launch (start us, length us, event | category | flops | bytes accessed | tf_op | source)
XLA Modules:
  0.0 320.8 jit_solution(7618125322044810644)
XLA Ops:
  0.6 0.0 copy-start.5
  0.7 0.0 copy-start.6
  0.7 0.0 copy-start.7
  0.7 0.0 copy-start.8
  0.7 0.0 copy-start.9
  0.7 0.0 copy-start.10
  0.7 0.0 copy-start.11
  0.7 0.0 copy-start.12
  0.7 1.1 copy.36
  1.9 1.6 pad_maximum_fusion.shard_one
  3.4 0.7 tile.20
  4.1 0.1 tile.21
  4.2 0.1 broadcast_in_dim.46
  4.3 0.7 tile.8
  5.0 0.1 tile.9
  5.2 0.1 pad.3.clone
  5.2 0.7 maximum_bitcast_fusion.small
  5.9 0.7 convert_multiply_fusion
  6.6 0.1 select_reduce_fusion
  6.7 2.8 add_convert_fusion.h
  9.5 0.0 copy-done.5
  9.5 0.0 copy-done.6
  9.5 0.0 copy-done.7
  9.5 0.0 copy-done.8
  9.5 0.0 copy-done.9
  9.5 0.0 copy-done.10
  9.5 0.0 copy-done.11
  9.5 0.0 copy-done.12
  9.6 0.7 stack.29.vecs
  10.2 142.9 %forward.1 = (bf16[4,8,4,256,128]{4,3,2,1,0:T(8,128)(2,1)}, bf16[4,8,4,256,128]{4,3,2,1,0:T(8,128)(2,1)}, bf16[4,8,4,256,128]{4,3,2,1,0:T(8,128)(2,1)}, bf16[4,1...) custom-call(s32[5]{0:T(128)} %context.3, ...), custom_call_target="tpu_custom_call" | custom-call | tf_op jit(solution)/shard_map/forward/pallas_call | solution.py:490
  153.1 156.3 %backward.1 = (f32[4,256,128]{2,1,0:T(8,128)}, f32[4,256,128]{2,1,0:T(8,128)}, f32[256,128]{1,0:T(8,128)}, f32[3,128,256]{2,1,0:T(8,128)}, f32[16,1024]{1,0:T(8,128)}, /*index=5*/f32[640,1024]{1,0:T(8,128)}) custom-call(s32[5]{0:T(128)} %context.3, s32[5]{0:T(128)} %timestep.3, bf16[4,8,4,256,128]{4,3,2,1,0:T(8,128)(2,1)} %get-tuple-element.41.w_one, ...), custom_call_target="tpu_custom_call" | custom-call | tf_op jit(solution)/shard_map/backward/pallas_call | solution.py:1003
  309.4 0.0 copy-start
  309.4 0.9 constant_dynamic-slice_fusion.2
  310.3 0.5 slice_bitcast_fusion
  310.9 0.8 slice.33
  311.7 0.1 reshape.97
  311.8 0.1 reshape.98
  311.8 0.7 dynamic_slice.13
  312.5 0.7 constant_dynamic-slice_fusion
  313.2 0.7 constant_dynamic-slice_fusion.1
  313.9 2.5 copy.44
  316.3 0.0 copy-done
  316.3 0.0 copy-start.3
  316.3 0.0 copy-start.4
  316.3 0.0 copy-start.2
  316.3 0.0 copy-start.1
  316.3 1.5 copy.45
  317.8 0.0 copy-done.3
  317.8 0.7 copy.46
  318.6 0.0 copy-done.4
  318.6 0.7 copy.47
  319.2 0.0 copy-done.2
  319.3 0.8 copy.48
  320.0 0.0 copy-done.1
  320.0 0.8 copy.49
  (10 shorter events, 0.1 us)
Async XLA Ops:
  0.6 8.9 %copy-start.5 = (f32[1024]{0:T(1024)S(1)}, f32[1024]{0:T(1024)}, u32[]{:S(2)}) copy-start(f32[1024]{0:T(1024)} %param.22) | copy-start | bytes 12292
  0.7 8.8 %copy-start.6 = (f32[1024]{0:T(1024)S(1)}, f32[1024]{0:T(1024)}, u32[]{:S(2)}) copy-start(f32[1024]{0:T(1024)} %param.21) | copy-start | bytes 12292
  0.7 8.8 %copy-start.7 = (f32[1024]{0:T(1024)S(1)}, f32[1024]{0:T(1024)}, u32[]{:S(2)}) copy-start(f32[1024]{0:T(1024)} %param.26) | copy-start | bytes 12292
  0.7 8.8 %copy-start.8 = (f32[1024]{0:T(1024)S(1)}, f32[1024]{0:T(1024)}, u32[]{:S(2)}) copy-start(f32[1024]{0:T(1024)} %param.27) | copy-start | bytes 12292
  0.7 8.8 %copy-start.9 = (f32[1024]{0:T(1024)S(1)}, f32[1024]{0:T(1024)}, u32[]{:S(2)}) copy-start(f32[1024]{0:T(1024)} %param.28) | copy-start | bytes 12292
  0.7 8.8 %copy-start.10 = (f32[1024]{0:T(1024)S(1)}, f32[1024]{0:T(1024)}, u32[]{:S(2)}) copy-start(f32[1024]{0:T(1024)} %param.32) | copy-start | bytes 12292
  0.7 8.8 %copy-start.11 = (f32[1024]{0:T(1024)S(1)}, f32[1024]{0:T(1024)}, u32[]{:S(2)}) copy-start(f32[1024]{0:T(1024)} %param.33) | copy-start | bytes 12292
  0.7 8.8 %copy-start.12 = (f32[1024]{0:T(1024)S(1)}, f32[1024]{0:T(1024)}, u32[]{:S(2)}) copy-start(f32[1024]{0:T(1024)} %param.34) | copy-start | bytes 12292
  309.4 6.9 %copy-start = (f32[640,1024]{1,0:T(8,128)S(1)}, f32[640,1024]{1,0:T(8,128)}, u32[]{:S(2)}) copy-start(f32[640,1024]{1,0:T(8,128)} %get-tuple-element.91) | copy-start | bytes 7864324
  316.3 1.5 copy-start.3
  316.3 2.3 copy-start.4
  316.3 2.9 copy-start.2
  316.3 3.7 %copy-start.1 = (f32[4,256,128]{2,1,0:T(8,128)S(1)}, f32[4,256,128]{2,1,0:T(8,128)}, u32[]{:S(2)}) copy-start(f32[4,256,128]{2,1,0:T(8,128)} %get-tuple-element.63) | copy-start | bytes 1572868

commit v2 on v1

--- a/solution.py
+++ b/solution.py
@@ -864,18 +864,19 @@
         tiles(one)
         get_weight(w_one.at[0], 1)
 
-        for i in range(3):
-            @pl.when(z > i)
-            def _():
-                src = h_win.at[tile_rows(i * step, step)]
-                dst = halo_in.at[tile_rows((5 - z + i) * step, step)]
-                send(src, dst, halo_sent, halo_got, at.along(3))
-
-            @pl.when(z < 3 - i)
-            def _():
-                src = h_win.at[tile_rows((5 + z + i) * step, step)]
-                dst = halo_in.at[tile_rows(i * step, step)]
-                send(src, dst, halo_sent, halo_got, at.along(1))
+    def halo(part):
+        i, half = part // 2, step // 2
+
+        def some_rows(start):
+            return pl.ds(pl.multiple_of(start * step + part % 2 * half, half), half)
+
+        @pl.when(z > i)
+        def _():
+            send(h_win.at[some_rows(i)], halo_in.at[some_rows(5 - z + i)], halo_sent, halo_got, at.along(3))
+
+        @pl.when(z < 3 - i)
+        def _():
+            send(h_win.at[some_rows(5 + z + i)], halo_in.at[some_rows(i)], halo_sent, halo_got, at.along(1))
 
     def input_own():
         have_weight(1)
@@ -935,15 +936,13 @@
             put_tokens(j).start()
 
     get(0).start()
-    for i in range(2):
-        for copy in get_hidden(i):
-            copy.start()
+    early = get_hidden(0)
+    early[0].start()
     get_weight(w_down.at[0], 0)
-    for i in range(1, 3):
-        get(i).start()
+    early[1].start()
+    get(1).start()
     get_weight(w_up.at[0], 1)
-    for i in range(3, 9):
-        get(i).start()
+    get(2).start()
     work = {
         5: (norm_one,),
         6: (grad_out, lambda: attend_pairs(0, 1)),
@@ -951,11 +950,11 @@
         8: (lambda: attend_pairs(4, 3),),
         9: (lambda: attend_pairs(7, 1), grad_value),
         10: (grad_key_query,),
-        11: (input_window,),
-        12: (input_own, lambda: small_send(0)),
-        13: (lambda: small_add(0), lambda: small_send(1)),
-        14: (lambda: small_add(1), lambda: small_send(2), finish_tokens),
-        15: (lambda: small_add(2), small_spread),
+        11: (input_window, lambda: halo(0), lambda: halo(1)),
+        12: (lambda: halo(2), lambda: halo(3), input_own, lambda: small_send(0)),
+        13: (lambda: halo(4), lambda: halo(5), lambda: small_add(0), lambda: small_send(1)),
+        14: (lambda: small_add(1), lambda: small_send(2)),
+        15: (lambda: small_add(2), small_spread, finish_tokens),
     }
 
     def slot_run(s, carry):
@@ -966,6 +965,21 @@
         def sub_step(u, inner):
             when_in(3 * s - 2 + u, 16, feed_forward)
             return inner
+
+        @pl.when(s == 1)
+        def _():
+            for copy in get_hidden(1):
+                copy.start()
+
+        @pl.when(s == 2)
+        def _():
+            for i in range(3, 5):
+                get(i).start()
+
+        @pl.when(s == 3)
+        def _():
+            for i in range(5, 9):
+                get(i).start()
 
         lax.fori_loop(0, 3, sub_step, 0)
 

time: 321 us -> 318 us (level)
  no operation moved by 1% of the time
where the time goes in v2:
time: 318 us
  Pallas kernels  296 us (93%)
  local copies, waits for them, and re-layouts  14.9 us (5%)
  other arithmetic  5.87 us (2%)
    pallas_call x1, Pallas kernels, backward_pass(): pl.pallas_call(functools.partial(backward_kernel, outer), out_shape=(jax....  153 us
    pallas_call x1, Pallas kernels, forward_pass(): pl.pallas_call(functools.partial(forward_kernel, outer), out_shape=(weigh...  143 us
    unnamed x33, local copies, waits for them, and re-layouts  8.13 us

profile of v2, /device:TPU:0, one launch (start us, length us, event | category | flops | bytes accessed | tf_op | source)
XLA Modules:
  0.0 317.7 jit_solution(13274486536921075177)
XLA Ops:
  0.6 0.0 copy-start.5
  0.7 0.0 copy-start.6
  0.7 0.0 copy-start.7
  0.7 0.0 copy-start.8
  0.7 0.0 copy-start.9
  0.7 0.0 copy-start.10
  0.7 0.0 copy-start.11
  0.7 0.0 copy-start.12
  0.7 1.1 copy.36
  1.9 1.6 pad_maximum_fusion.shard_one
  3.4 0.7 tile.20
  4.1 0.1 tile.21
  4.2 0.1 broadcast_in_dim.46
  4.3 0.7 tile.8
  5.0 0.1 tile.9
  5.2 0.1 pad.3.clone
  5.2 0.7 maximum_bitcast_fusion.small
  5.9 0.7 convert_multiply_fusion
  6.6 0.1 select_reduce_fusion
  6.7 2.8 add_convert_fusion.h
  9.5 0.0 copy-done.5
  9.5 0.0 copy-done.6
  9.5 0.0 copy-done.7
  9.5 0.0 copy-done.8
  9.5 0.0 copy-done.9
  9.5 0.0 copy-done.10
  9.5 0.0 copy-done.11
  9.5 0.0 copy-done.12
  9.6 0.7 stack.29.vecs
  10.2 142.9 %forward.1 = (bf16[4,8,4,256,128]{4,3,2,1,0:T(8,128)(2,1)}, bf16[4,8,4,256,128]{4,3,2,1,0:T(8,128)(2,1)}, bf16[4,8,4,256,128]{4,3,2,1,0:T(8,128)(2,1)}, bf16[4,1...) custom-call(s32[5]{0:T(128)} %context.3, ...), custom_call_target="tpu_custom_call" | custom-call | tf_op jit(solution)/shard_map/forward/pallas_call | solution.py:490
  153.1 153.1 %backward.1 = (f32[4,256,128]{2,1,0:T(8,128)}, f32[4,256,128]{2,1,0:T(8,128)}, f32[256,128]{1,0:T(8,128)}, f32[3,128,256]{2,1,0:T(8,128)}, f32[16,1024]{1,0:T(8,128)}, /*index=5*/f32[640,1024]{1,0:T(8,128)}) custom-call(s32[5]{0:T(128)} %context.3, s32[5]{0:T(128)} %timestep.3, bf16[4,8,4,256,128]{4,3,2,1,0:T(8,128)(2,1)} %get-tuple-element.41.w_one, ...), custom_call_target="tpu_custom_call" | custom-call | tf_op jit(solution)/shard_map/backward/pallas_call | solution.py:1017
  306.3 0.0 copy-start
  306.3 0.9 constant_dynamic-slice_fusion.2
  307.2 0.5 slice_bitcast_fusion
  307.7 0.8 slice.33
  308.5 0.1 reshape.97
  308.6 0.1 reshape.98
  308.7 0.7 dynamic_slice.13
  309.3 0.7 constant_dynamic-slice_fusion
  310.0 0.7 constant_dynamic-slice_fusion.1
  310.7 2.5 copy.44
  313.2 0.0 copy-done
  313.2 0.0 copy-start.3
  313.2 0.0 copy-start.4
  313.2 0.0 copy-start.2
  313.2 0.0 copy-start.1
  313.2 1.5 copy.45
  314.7 0.0 copy-done.3
  314.7 0.7 copy.46
  315.4 0.0 copy-done.4
  315.4 0.7 copy.47
  316.1 0.0 copy-done.2
  316.1 0.8 copy.48
  316.9 0.0 copy-done.1
  316.9 0.8 copy.49
  (10 shorter events, 0.1 us)
Async XLA Ops:
  0.6 8.9 %copy-start.5 = (f32[1024]{0:T(1024)S(1)}, f32[1024]{0:T(1024)}, u32[]{:S(2)}) copy-start(f32[1024]{0:T(1024)} %param.22) | copy-start | bytes 12292
  0.7 8.8 %copy-start.6 = (f32[1024]{0:T(1024)S(1)}, f32[1024]{0:T(1024)}, u32[]{:S(2)}) copy-start(f32[1024]{0:T(1024)} %param.21) | copy-start | bytes 12292
  0.7 8.8 %copy-start.7 = (f32[1024]{0:T(1024)S(1)}, f32[1024]{0:T(1024)}, u32[]{:S(2)}) copy-start(f32[1024]{0:T(1024)} %param.26) | copy-start | bytes 12292
  0.7 8.8 %copy-start.8 = (f32[1024]{0:T(1024)S(1)}, f32[1024]{0:T(1024)}, u32[]{:S(2)}) copy-start(f32[1024]{0:T(1024)} %param.27) | copy-start | bytes 12292
  0.7 8.8 %copy-start.9 = (f32[1024]{0:T(1024)S(1)}, f32[1024]{0:T(1024)}, u32[]{:S(2)}) copy-start(f32[1024]{0:T(1024)} %param.28) | copy-start | bytes 12292
  0.7 8.8 %copy-start.10 = (f32[1024]{0:T(1024)S(1)}, f32[1024]{0:T(1024)}, u32[]{:S(2)}) copy-start(f32[1024]{0:T(1024)} %param.32) | copy-start | bytes 12292
  0.7 8.8 %copy-start.11 = (f32[1024]{0:T(1024)S(1)}, f32[1024]{0:T(1024)}, u32[]{:S(2)}) copy-start(f32[1024]{0:T(1024)} %param.33) | copy-start | bytes 12292
  0.7 8.8 %copy-start.12 = (f32[1024]{0:T(1024)S(1)}, f32[1024]{0:T(1024)}, u32[]{:S(2)}) copy-start(f32[1024]{0:T(1024)} %param.34) | copy-start | bytes 12292
  306.3 6.9 %copy-start = (f32[640,1024]{1,0:T(8,128)S(1)}, f32[640,1024]{1,0:T(8,128)}, u32[]{:S(2)}) copy-start(f32[640,1024]{1,0:T(8,128)} %get-tuple-element.91) | copy-start | bytes 7864324
  313.2 1.5 copy-start.3
  313.2 2.3 copy-start.4
  313.2 2.9 copy-start.2
  313.2 3.7 %copy-start.1 = (f32[4,256,128]{2,1,0:T(8,128)S(1)}, f32[4,256,128]{2,1,0:T(8,128)}, u32[]{:S(2)}) copy-start(f32[4,256,128]{2,1,0:T(8,128)} %get-tuple-element.63) | copy-start | bytes 1572868

commit v3 on v2

--- a/solution.py
+++ b/solution.py
@@ -329,7 +329,7 @@
         store(attn, attn_out)
 
         def norm(here, i):
-            share = timestep[z + lax.div(z + lax.div(i * 32, step), 4)].astype(F32) * (1.0 / TSTEPS)
+            share = timestep[z + lax.div(z + lax.div(i * 64, step), 4)].astype(F32) * (1.0 / TSTEPS)
             h_zero = tokens[here, :].astype(F32) + share * vecs[0:1, :] + vecs[1:2, :]
             normal, rstd = norm_rows(h_zero + acc[here, :] + vecs[2:3, :])
             xhat[here, :] = normal
@@ -337,10 +337,10 @@
             rstd_out[here, :] = jnp.broadcast_to(rstd, (rstd.shape[0], COLS))
 
         def run(i, carry):
-            norm(pl.ds(pl.multiple_of(i * 32, 32), 32), i)
+            norm(pl.ds(pl.multiple_of(i * 64, 64), 64), i)
             return carry
 
-        lax.fori_loop(0, rows // 32, run, 0)
+        lax.fori_loop(0, rows // 64, run, 0)
         acc[...] = jnp.zeros_like(acc)
         store(y_low, y_out)
         store(xhat, xhat_out)
@@ -371,7 +371,7 @@
                 hidden[i, here, span] = (x * cdf).astype(BF)
                 slope[side, here, span] = (cdf + x * pdf).astype(BF)
 
-            row_loop(32, gelu)
+            row_loop(64, gelu)
 
         tiles(one)
         slope_store(i).start()
@@ -402,7 +402,7 @@
             sums[1] += fold_rows(cot)
             sums[2] += fold_rows(low.astype(F32))
 
-        row_loop(32, norm)
+        row_loop(128, norm)
         store(acc, dz_out)
         store(grad_f, grad_f_out)
         store(out_rows, layer_out)
@@ -794,7 +794,7 @@
             grad_f[here, :] = low
             stats[2] += fold_rows(low.astype(F32))
 
-        row_loop(32, back)
+        row_loop(64, back)
 
     def grad_out():
         produce(8, attn, lambda: grad_f[...])

time: 318 us -> 311 us (0.978)
  Pallas kernels: 296 us -> 289 us
    pallas_call x1, Pallas kernels: 143 us -> 137 us  [forward_pass(): pl.pallas_call(functools.partial(forward_kernel, outer), out_shape=(weigh...]
where the time goes in v3:
time: 311 us
  Pallas kernels  289 us (93%)
  local copies, waits for them, and re-layouts  14.9 us (5%)
  other arithmetic  5.87 us (2%)
    pallas_call x1, Pallas kernels, backward_pass(): pl.pallas_call(functools.partial(backward_kernel, outer), out_shape=(jax....  152 us
    pallas_call x1, Pallas kernels, forward_pass(): pl.pallas_call(functools.partial(forward_kernel, outer), out_shape=(weigh...  137 us
    unnamed x33, local copies, waits for them, and re-layouts  8.13 us

profile of v3, /device:TPU:0, one launch (start us, length us, event | category | flops | bytes accessed | tf_op | source)
XLA Modules:
  0.0 310.8 jit_solution(239176666535626343)
XLA Ops:
  0.6 0.0 copy-start.5
  0.7 0.0 copy-start.6
  0.7 0.0 copy-start.7
  0.7 0.0 copy-start.8
  0.7 0.0 copy-start.9
  0.7 0.0 copy-start.10
  0.7 0.0 copy-start.11
  0.7 0.0 copy-start.12
  0.7 1.1 copy.36
  1.9 1.6 pad_maximum_fusion.shard_one
  3.4 0.7 tile.20
  4.1 0.1 tile.21
  4.2 0.1 broadcast_in_dim.46
  4.3 0.7 tile.8
  5.0 0.1 tile.9
  5.2 0.1 pad.3.clone
  5.2 0.7 maximum_bitcast_fusion.small
  5.9 0.7 convert_multiply_fusion
  6.6 0.1 select_reduce_fusion
  6.7 2.8 add_convert_fusion.h
  9.5 0.0 copy-done.5
  9.5 0.0 copy-done.6
  9.5 0.0 copy-done.7
  9.5 0.0 copy-done.8
  9.5 0.0 copy-done.9
  9.5 0.0 copy-done.10
  9.5 0.0 copy-done.11
  9.5 0.0 copy-done.12
  9.6 0.7 stack.29.vecs
  10.2 136.9 %forward.1 = (bf16[4,8,4,256,128]{4,3,2,1,0:T(8,128)(2,1)}, bf16[4,8,4,256,128]{4,3,2,1,0:T(8,128)(2,1)}, bf16[4,8,4,256,128]{4,3,2,1,0:T(8,128)(2,1)}, bf16[4,1...) custom-call(s32[5]{0:T(128)} %context.3, ...), custom_call_target="tpu_custom_call" | custom-call | tf_op jit(solution)/shard_map/forward/pallas_call | solution.py:490
  147.1 152.3 %backward.1 = (f32[4,256,128]{2,1,0:T(8,128)}, f32[4,256,128]{2,1,0:T(8,128)}, f32[256,128]{1,0:T(8,128)}, f32[3,128,256]{2,1,0:T(8,128)}, f32[16,1024]{1,0:T(8,128)}, /*index=5*/f32[640,1024]{1,0:T(8,128)}) custom-call(s32[5]{0:T(128)} %context.3, s32[5]{0:T(128)} %timestep.3, bf16[4,8,4,256,128]{4,3,2,1,0:T(8,128)(2,1)} %get-tuple-element.41.w_one, ...), custom_call_target="tpu_custom_call" | custom-call | tf_op jit(solution)/shard_map/backward/pallas_call | solution.py:1017
  299.4 0.0 copy-start
  299.4 0.9 constant_dynamic-slice_fusion.2
  300.3 0.5 slice_bitcast_fusion
  300.9 0.8 slice.33
  301.6 0.1 reshape.97
  301.7 0.1 reshape.98
  301.8 0.7 dynamic_slice.13
  302.5 0.7 constant_dynamic-slice_fusion
  303.2 0.7 constant_dynamic-slice_fusion.1
  303.9 2.5 copy.44
  306.3 0.0 copy-done
  306.3 0.0 copy-start.3
  306.3 0.0 copy-start.4
  306.3 0.0 copy-start.2
  306.3 0.0 copy-start.1
  306.3 1.5 copy.45
  307.8 0.0 copy-done.3
  307.8 0.7 copy.46
  308.6 0.0 copy-done.4
  308.6 0.7 copy.47
  309.2 0.0 copy-done.2
  309.2 0.8 copy.48
  310.0 0.0 copy-done.1
  310.0 0.8 copy.49
  (10 shorter events, 0.1 us)
Async XLA Ops:
  0.6 8.9 %copy-start.5 = (f32[1024]{0:T(1024)S(1)}, f32[1024]{0:T(1024)}, u32[]{:S(2)}) copy-start(f32[1024]{0:T(1024)} %param.22) | copy-start | bytes 12292
  0.7 8.8 %copy-start.6 = (f32[1024]{0:T(1024)S(1)}, f32[1024]{0:T(1024)}, u32[]{:S(2)}) copy-start(f32[1024]{0:T(1024)} %param.21) | copy-start | bytes 12292
  0.7 8.8 %copy-start.7 = (f32[1024]{0:T(1024)S(1)}, f32[1024]{0:T(1024)}, u32[]{:S(2)}) copy-start(f32[1024]{0:T(1024)} %param.26) | copy-start | bytes 12292
  0.7 8.8 %copy-start.8 = (f32[1024]{0:T(1024)S(1)}, f32[1024]{0:T(1024)}, u32[]{:S(2)}) copy-start(f32[1024]{0:T(1024)} %param.27) | copy-start | bytes 12292
  0.7 8.8 %copy-start.9 = (f32[1024]{0:T(1024)S(1)}, f32[1024]{0:T(1024)}, u32[]{:S(2)}) copy-start(f32[1024]{0:T(1024)} %param.28) | copy-start | bytes 12292
  0.7 8.8 %copy-start.10 = (f32[1024]{0:T(1024)S(1)}, f32[1024]{0:T(1024)}, u32[]{:S(2)}) copy-start(f32[1024]{0:T(1024)} %param.32) | copy-start | bytes 12292
  0.7 8.8 %copy-start.11 = (f32[1024]{0:T(1024)S(1)}, f32[1024]{0:T(1024)}, u32[]{:S(2)}) copy-start(f32[1024]{0:T(1024)} %param.33) | copy-start | bytes 12292
  0.7 8.8 %copy-start.12 = (f32[1024]{0:T(1024)S(1)}, f32[1024]{0:T(1024)}, u32[]{:S(2)}) copy-start(f32[1024]{0:T(1024)} %param.34) | copy-start | bytes 12292
  299.4 6.9 %copy-start = (f32[640,1024]{1,0:T(8,128)S(1)}, f32[640,1024]{1,0:T(8,128)}, u32[]{:S(2)}) copy-start(f32[640,1024]{1,0:T(8,128)} %get-tuple-element.91) | copy-start | bytes 7864324
  306.3 1.5 copy-start.3
  306.3 2.3 copy-start.4
  306.3 2.9 copy-start.2
  306.3 3.7 %copy-start.1 = (f32[4,256,128]{2,1,0:T(8,128)S(1)}, f32[4,256,128]{2,1,0:T(8,128)}, u32[]{:S(2)}) copy-start(f32[4,256,128]{2,1,0:T(8,128)} %get-tuple-element.63) | copy-start | bytes 1572868
